TPU v7x, 32 devices: a whole 2x2x4 slice. The times are simulated.
32 devices in a mesh: ctx: 8 (over y, x, core), fsdp: 4 (over z).
Axes of the slice: x: 2, y: 2, z: 4, core: 2. Of those that a mesh axis runs over, the one named last changes fastest.
Arguments:
- tokens: bfloat16 [4, 2048, 768], P('fsdp', 'ctx'), may hold values from -6 to 6
- segments: int32 [4, 2048], P('fsdp'), may hold values from 0 to 15, never falling along the last dimension, each value on 1 to 1536 neighbouring positions
- w_query: bfloat16 [768, 768], P('fsdp'), may hold values from -0.3125 to 0.3125
- b_query: bfloat16 [768], P('fsdp'), may hold values from -3 to 3
- w_key: bfloat16 [768, 768], P('fsdp'), may hold values from -0.3125 to 0.3125
- w_value: bfloat16 [768, 768], P('fsdp'), may hold values from -0.21875 to 0.21875
- b_value: bfloat16 [768], P('fsdp'), may hold values from -3 to 3
- w_out: bfloat16 [768, 768], P('fsdp'), may hold values from -1.75 to 1.75
- b_out: bfloat16 [768], P('fsdp'), may hold values from -3 to 3
- gain_attention: bfloat16 [768], P('fsdp'), may hold values from 0.099609375 to 1.8984375
- bias_attention: bfloat16 [768], P('fsdp'), may hold values from -3 to 3
- w_inner: bfloat16 [768, 3072], P('fsdp'), may hold values from -0.21875 to 0.21875
- b_inner: bfloat16 [3072], P('fsdp'), may hold values from -3 to 3
- w_outer: bfloat16 [3072, 768], P('fsdp'), may hold values from -0.109375 to 0.109375
- b_outer: bfloat16 [768], P('fsdp'), may hold values from -3 to 3
- gain_feed: bfloat16 [768], P('fsdp'), may hold values from 0.099609375 to 1.8984375
- bias_feed: bfloat16 [768], P('fsdp'), may hold values from -3 to 3
- cotangent: bfloat16 [4, 2048, 768], P('fsdp', 'ctx'), may hold values from -6 to 6
Outputs:
- output: bfloat16 [4, 2048, 768], P('fsdp', 'ctx')
- grad_input: float32 [4, 2048, 768], P('fsdp', 'ctx')
- grad_w_query: float32 [768, 768], P('fsdp')
- grad_b_query: float32 [768], P('fsdp')
- grad_w_key: float32 [768, 768], P('fsdp')
- grad_w_value: float32 [768, 768], P('fsdp')
- grad_b_value: float32 [768], P('fsdp')
- grad_w_out: float32 [768, 768], P('fsdp')
- grad_b_out: float32 [768], P('fsdp')
- grad_gain_attention: float32 [768], P('fsdp')
- grad_bias_attention: float32 [768], P('fsdp')
- grad_w_inner: float32 [768, 3072], P('fsdp')
- grad_b_inner: float32 [3072], P('fsdp')
- grad_w_outer: float32 [3072, 768], P('fsdp')
- grad_b_outer: float32 [768], P('fsdp')
- grad_gain_feed: float32 [768], P('fsdp')
- grad_bias_feed: float32 [768], P('fsdp')
Inputs may be any that keep to these rules, and one draw needn't show every extreme that they name: `segments`: along a sequence the document numbers never fall; each document has 1 to 1536 tokens, and one has exactly 1536.
All inputs are finite; a program needn't handle non-finite values.
Results may differ from a plain program's by a relative error of at most 0.023.
Values may be sent and summed in bfloat16 or wider, within the bound.
No kernel may reach another device: no remote copies, remote signals or barrier semaphores. Data moves between devices by JAX's collectives and lax.ppermute only.
A program may use at most 128 MiB of HBM per device.

v0:
```python
import math

import jax
import jax.numpy as jnp
from jax import lax
from jax.sharding import PartitionSpec as P

HEADS = 12


ln_epsilon = 1e-12


def from_behind(block, axis, distance):
    devices = range(lax.axis_size(axis))
    route = [((i - distance) % len(devices), i) for i in devices]
    return lax.ppermute(block, axis, route)


def shortened(x):
    return jax.tree.map(lambda a: a.astype(jnp.bfloat16) if a.dtype == jnp.float32 else a, x)


def layer_norm(values, gain, bias):
    center = values - jnp.mean(values, axis=-1, keepdims=True)
    spread = jnp.mean(center * center, axis=-1, keepdims=True)
    return center * lax.rsqrt(spread + ln_epsilon) * gain + bias


def gelu_exact(values):
    return jax.nn.gelu(values, approximate=False)


def linear(left, right):
    return jnp.dot(left, right, preferred_element_type=jnp.float32)


def per_device(
    tokens,
    segments,
    w_query,
    b_query,
    w_key,
    w_value,
    b_value,
    w_out,
    b_out,
    gain_attention,
    bias_attention,
    w_inner,
    b_inner,
    w_outer,
    b_outer,
    gain_feed,
    bias_feed,
    cotangent,
):
    seqs_here = tokens.shape[0]
    rows = tokens.shape[1]
    width = tokens.shape[2]
    heads = HEADS
    head_size = width // heads
    cycle = lax.axis_size("ctx")
    place = lax.axis_index("ctx")
    inputs = tokens.reshape(seqs_here * rows, width)
    seg_own = lax.dynamic_slice_in_dim(segments, place * rows, rows, axis=1)
    f32 = jnp.float32
    b16 = jnp.bfloat16
    attention_set = (
        lax.all_gather(w_query, "fsdp", axis=0, tiled=True),
        lax.all_gather(w_key, "fsdp", axis=0, tiled=True),
        lax.all_gather(w_value, "fsdp", axis=0, tiled=True),
        lax.all_gather(w_out, "fsdp", axis=0, tiled=True),
        lax.all_gather(b_query, "fsdp", axis=0, tiled=True),
        lax.all_gather(b_value, "fsdp", axis=0, tiled=True),
        lax.all_gather(b_out, "fsdp", axis=0, tiled=True),
        lax.all_gather(gain_attention, "fsdp", axis=0, tiled=True),
        lax.all_gather(bias_attention, "fsdp", axis=0, tiled=True),
    )
    feed_set = (
        lax.all_gather(w_inner, "fsdp", axis=0, tiled=True),
        lax.all_gather(w_outer, "fsdp", axis=0, tiled=True),
        lax.all_gather(b_inner, "fsdp", axis=0, tiled=True),
        lax.all_gather(b_outer, "fsdp", axis=0, tiled=True),
        lax.all_gather(gain_feed, "fsdp", axis=0, tiled=True),
        lax.all_gather(bias_feed, "fsdp", axis=0, tiled=True),
    )
    (
        query_matrix,
        key_matrix,
        value_matrix,
        out_matrix,
        query_shift,
        value_shift,
        out_shift,
        first_gain,
        first_bias,
    ) = attention_set
    inner_matrix, outer_matrix, inner_shift, outer_shift, second_gain, second_bias = feed_set
    query = (linear(inputs, query_matrix) + query_shift.astype(f32)).astype(b16)
    keys = linear(inputs, key_matrix).astype(b16).reshape(seqs_here, rows, width)
    values = (
        (linear(inputs, value_matrix) + value_shift.astype(f32))
        .astype(b16)
        .reshape(seqs_here, rows, width)
    )
    query_heads = query.reshape(seqs_here, rows, heads, head_size)

    def scored(query_rows, key_rows, seg_query, seg_keys):
        key_heads = key_rows.reshape(key_rows.shape[0], key_rows.shape[1], heads, head_size)
        scores = (
            jnp.einsum("sthd,srhd->shtr", query_rows, key_heads, preferred_element_type=f32) * 0.125
        )
        allowed = (seg_query[:, :, None] == seg_keys[:, None, :])[:, None]
        return (scores, allowed)

    def over_blocks(piece, carry, action):
        count = jax.tree.leaves(piece)[0].shape[1]
        block = math.gcd(count, rows)

        def turn(number, state):
            offset = number * block
            part = jax.tree.map(
                lambda whole: lax.dynamic_slice_in_dim(whole, offset, block, axis=1), piece
            )
            seg_keys = lax.dynamic_slice_in_dim(segments, offset, block, axis=1)
            return action(state, part, seg_keys)

        return lax.fori_loop(0, count // block, turn, carry)

    def stat_action(state, key_rows, seg_keys):
        peak, total = state
        scores, allowed = scored(query_heads, key_rows, seg_own, seg_keys)
        masked = jnp.where(allowed, scores, -1e30)
        top = jnp.maximum(peak, jnp.max(masked, axis=-1))
        terms = jnp.where(allowed, jnp.exp(masked - top[..., None]), 0.0)
        return (top, total * jnp.exp(peak - top) + jnp.sum(terms, axis=-1))

    start_stats = (
        jnp.full((seqs_here, heads, rows), -1e30, f32),
        jnp.zeros((seqs_here, heads, rows), f32),
    )
    peak, total = over_blocks(
        lax.all_gather(keys, "ctx", axis=1, tiled=True), start_stats, stat_action
    )
    log_total = peak + jnp.log(total)

    def probs_of(scores, allowed, log_rows):
        return jnp.where(
            allowed, jnp.exp(jnp.where(allowed, scores, -1e30) - log_rows[..., None]), 0.0
        )

    def value_action(state, pair, seg_keys):
        key_rows, value_rows = pair
        scores, allowed = scored(query_heads, key_rows, seg_own, seg_keys)
        weights = probs_of(scores, allowed, log_total).astype(b16)
        value_heads = value_rows.reshape(value_rows.shape[0], value_rows.shape[1], heads, head_size)
        return state + jnp.einsum(
            "shtr,srhd->sthd", weights, value_heads, preferred_element_type=f32
        )

    attended = over_blocks(
        (
            lax.all_gather(keys, "ctx", axis=1, tiled=True),
            lax.all_gather(values, "ctx", axis=1, tiled=True),
        ),
        jnp.zeros((seqs_here, rows, heads, head_size), f32),
        value_action,
    )
    attended_low = attended.reshape(seqs_here * rows, width).astype(b16)
    resid_one = inputs.astype(f32) + linear(attended_low, out_matrix) + out_shift.astype(f32)
    normed = layer_norm(resid_one, first_gain.astype(f32), first_bias.astype(f32))
    normed_low = normed.astype(b16)
    inner = linear(normed_low, inner_matrix) + inner_shift.astype(f32)
    active = gelu_exact(inner).astype(b16)
    resid_two = normed + linear(active, outer_matrix) + outer_shift.astype(f32)
    result = layer_norm(resid_two, second_gain.astype(f32), second_bias.astype(f32))
    attention_back = (
        lax.all_gather(w_query, "fsdp", axis=0, tiled=True),
        lax.all_gather(w_key, "fsdp", axis=0, tiled=True),
        lax.all_gather(w_value, "fsdp", axis=0, tiled=True),
        lax.all_gather(w_out, "fsdp", axis=0, tiled=True),
        lax.all_gather(b_query, "fsdp", axis=0, tiled=True),
        lax.all_gather(b_value, "fsdp", axis=0, tiled=True),
        lax.all_gather(b_out, "fsdp", axis=0, tiled=True),
        lax.all_gather(gain_attention, "fsdp", axis=0, tiled=True),
        lax.all_gather(bias_attention, "fsdp", axis=0, tiled=True),
    )
    feed_back = (
        lax.all_gather(w_inner, "fsdp", axis=0, tiled=True),
        lax.all_gather(w_outer, "fsdp", axis=0, tiled=True),
        lax.all_gather(b_inner, "fsdp", axis=0, tiled=True),
        lax.all_gather(b_outer, "fsdp", axis=0, tiled=True),
        lax.all_gather(gain_feed, "fsdp", axis=0, tiled=True),
        lax.all_gather(bias_feed, "fsdp", axis=0, tiled=True),
    )
    query_back, key_back, value_back, out_back = (
        attention_back[0],
        attention_back[1],
        attention_back[2],
        attention_back[3],
    )
    gain_one_back = attention_back[7].astype(f32)
    bias_one_back = attention_back[8].astype(f32)
    inner_back, outer_back = (feed_back[0], feed_back[1])
    gain_two_back = feed_back[4].astype(f32)
    bias_two_back = feed_back[5].astype(f32)
    upstream = cotangent.reshape(seqs_here * rows, width).astype(f32)
    unused_two, pull_two = jax.vjp(layer_norm, resid_two, gain_two_back, bias_two_back)
    grad_two, grad_gain_feed, grad_bias_feed = pull_two(upstream)
    grad_outer_low = grad_two.astype(b16)
    grad_b_outer = jnp.sum(grad_outer_low.astype(f32), axis=0)
    grad_w_outer = jnp.einsum("tf,td->fd", active, grad_outer_low, preferred_element_type=f32)
    grad_active = jnp.einsum("td,fd->tf", grad_outer_low, outer_back, preferred_element_type=f32)
    unused_gelu, pull_gelu = jax.vjp(gelu_exact, inner)
    grad_inner_low = pull_gelu(grad_active)[0].astype(b16)
    grad_b_inner = jnp.sum(grad_inner_low.astype(f32), axis=0)
    grad_w_inner = jnp.einsum("td,tf->df", normed_low, grad_inner_low, preferred_element_type=f32)
    grad_normed = grad_two + jnp.einsum(
        "tf,df->td", grad_inner_low, inner_back, preferred_element_type=f32
    )
    unused_one, pull_one = jax.vjp(layer_norm, resid_one, gain_one_back, bias_one_back)
    grad_one, grad_gain_attention, grad_bias_attention = pull_one(grad_normed)
    grad_branch_low = grad_one.astype(b16)
    grad_b_out = jnp.sum(grad_branch_low.astype(f32), axis=0)
    grad_w_out = jnp.einsum("td,te->de", attended_low, grad_branch_low, preferred_element_type=f32)
    grad_attended = jnp.einsum(
        "te,de->td", grad_branch_low, out_back, preferred_element_type=f32
    ).astype(b16)
    grad_heads = grad_attended.reshape(seqs_here, rows, heads, head_size)
    balance = jnp.swapaxes(jnp.sum(grad_heads.astype(f32) * attended, axis=-1), 1, 2)

    def back_block(
        query_rows, grad_rows, log_rows, balance_rows, seg_query, key_rows, value_rows, seg_keys
    ):
        scores, allowed = scored(query_rows, key_rows, seg_query, seg_keys)
        probs = probs_of(scores, allowed, log_rows)
        key_heads = key_rows.reshape(key_rows.shape[0], key_rows.shape[1], heads, head_size)
        value_heads = value_rows.reshape(value_rows.shape[0], value_rows.shape[1], heads, head_size)
        grad_probs = jnp.einsum(
            "sthd,srhd->shtr", grad_rows, value_heads, preferred_element_type=f32
        )
        grad_scores = (probs * (grad_probs - balance_rows[..., None])).astype(b16)
        part_query = (
            jnp.einsum("shtr,srhd->sthd", grad_scores, key_heads, preferred_element_type=f32)
            * 0.125
        )
        part_keys = (
            jnp.einsum("shtr,sthd->srhd", grad_scores, query_rows, preferred_element_type=f32)
            * 0.125
        )
        part_values = jnp.einsum(
            "shtr,sthd->srhd", probs.astype(b16), grad_rows, preferred_element_type=f32
        )
        return (
            part_query,
            part_keys.reshape(seqs_here, -1, width),
            part_values.reshape(seqs_here, -1, width),
        )

    zero_rows = jnp.zeros((seqs_here, rows, width), f32)
    zero_heads = jnp.zeros((seqs_here, rows, heads, head_size), f32)

    def key_turn(number, state):
        key_rows, value_rows, grad_keys, grad_values, grad_query = state
        anchor = (place - number) % cycle
        seg_keys = lax.dynamic_slice_in_dim(segments, anchor * rows, rows, axis=1)
        part_query, part_keys, part_values = back_block(
            query_heads, grad_heads, log_total, balance, seg_own, key_rows, value_rows, seg_keys
        )
        key_rows, value_rows = from_behind((key_rows, value_rows), "ctx", 1)
        grad_keys, grad_values = (
            from_behind((grad_keys + part_keys).astype(jnp.bfloat16), "ctx", 1).astype(jnp.float32),
            from_behind((grad_values + part_values).astype(jnp.bfloat16), "ctx", 1).astype(
                jnp.float32
            ),
        )
        return (key_rows, value_rows, grad_keys, grad_values, grad_query + part_query)

    final = lax.fori_loop(0, cycle, key_turn, (keys, values, zero_rows, zero_rows, zero_heads))
    grad_keys, grad_values, grad_query = (final[2], final[3], final[4])
    grad_query_low = grad_query.reshape(seqs_here * rows, width).astype(b16)
    grad_keys_low = grad_keys.reshape(seqs_here * rows, width).astype(b16)
    grad_values_low = grad_values.reshape(seqs_here * rows, width).astype(b16)
    grad_w_query = jnp.einsum("td,te->de", inputs, grad_query_low, preferred_element_type=f32)
    grad_b_query = jnp.sum(grad_query_low.astype(f32), axis=0)
    grad_w_key = jnp.einsum("td,te->de", inputs, grad_keys_low, preferred_element_type=f32)
    grad_w_value = jnp.einsum("td,te->de", inputs, grad_values_low, preferred_element_type=f32)
    grad_b_value = jnp.sum(grad_values_low.astype(f32), axis=0)
    grad_input = grad_one + jnp.einsum(
        "te,de->td", grad_query_low, query_back, preferred_element_type=f32
    )
    grad_input = grad_input + jnp.einsum(
        "te,de->td", grad_keys_low, key_back, preferred_element_type=f32
    )
    grad_input = grad_input + jnp.einsum(
        "te,de->td", grad_values_low, value_back, preferred_element_type=f32
    )
    shards = (
        lax.psum_scatter(
            grad_w_query.astype(jnp.bfloat16), "fsdp", scatter_dimension=0, tiled=True
        ).astype(jnp.float32),
        lax.psum_scatter(
            grad_b_query.astype(jnp.bfloat16), "fsdp", scatter_dimension=0, tiled=True
        ).astype(jnp.float32),
        lax.psum_scatter(
            grad_w_key.astype(jnp.bfloat16), "fsdp", scatter_dimension=0, tiled=True
        ).astype(jnp.float32),
        lax.psum_scatter(
            grad_w_value.astype(jnp.bfloat16), "fsdp", scatter_dimension=0, tiled=True
        ).astype(jnp.float32),
        lax.psum_scatter(
            grad_b_value.astype(jnp.bfloat16), "fsdp", scatter_dimension=0, tiled=True
        ).astype(jnp.float32),
        lax.psum_scatter(
            grad_w_out.astype(jnp.bfloat16), "fsdp", scatter_dimension=0, tiled=True
        ).astype(jnp.float32),
        lax.psum_scatter(
            grad_b_out.astype(jnp.bfloat16), "fsdp", scatter_dimension=0, tiled=True
        ).astype(jnp.float32),
        lax.psum_scatter(
            grad_gain_attention.astype(jnp.bfloat16), "fsdp", scatter_dimension=0, tiled=True
        ).astype(jnp.float32),
        lax.psum_scatter(
            grad_bias_attention.astype(jnp.bfloat16), "fsdp", scatter_dimension=0, tiled=True
        ).astype(jnp.float32),
        lax.psum_scatter(
            grad_w_inner.astype(jnp.bfloat16), "fsdp", scatter_dimension=0, tiled=True
        ).astype(jnp.float32),
        lax.psum_scatter(
            grad_b_inner.astype(jnp.bfloat16), "fsdp", scatter_dimension=0, tiled=True
        ).astype(jnp.float32),
        lax.psum_scatter(
            grad_w_outer.astype(jnp.bfloat16), "fsdp", scatter_dimension=0, tiled=True
        ).astype(jnp.float32),
        lax.psum_scatter(
            grad_b_outer.astype(jnp.bfloat16), "fsdp", scatter_dimension=0, tiled=True
        ).astype(jnp.float32),
        lax.psum_scatter(
            grad_gain_feed.astype(jnp.bfloat16), "fsdp", scatter_dimension=0, tiled=True
        ).astype(jnp.float32),
        lax.psum_scatter(
            grad_bias_feed.astype(jnp.bfloat16), "fsdp", scatter_dimension=0, tiled=True
        ).astype(jnp.float32),
    )
    totals = jax.tree.map(
        lambda part: part.astype(jnp.float32), lax.psum(shortened(tuple(shards)), "ctx")
    )
    output_rows = result.astype(b16).reshape(seqs_here, rows, width)
    grad_rows_out = grad_input.reshape(seqs_here, rows, width)
    return (output_rows, grad_rows_out) + tuple(totals)


def solution(mesh):
    return jax.shard_map(
        per_device,
        mesh=mesh,
        in_specs=(
            P("fsdp", "ctx", None),
            P("fsdp", None),
            P("fsdp", None),
            P("fsdp"),
            P("fsdp", None),
            P("fsdp", None),
            P("fsdp"),
            P("fsdp", None),
            P("fsdp"),
            P("fsdp"),
            P("fsdp"),
            P("fsdp", None),
            P("fsdp"),
            P("fsdp", None),
            P("fsdp"),
            P("fsdp"),
            P("fsdp"),
            P("fsdp", "ctx", None),
        ),
        out_specs=(
            P("fsdp", "ctx", None),
            P("fsdp", "ctx", None),
            P("fsdp", None),
            P("fsdp"),
            P("fsdp", None),
            P("fsdp", None),
            P("fsdp"),
            P("fsdp", None),
            P("fsdp"),
            P("fsdp"),
            P("fsdp"),
            P("fsdp", None),
            P("fsdp"),
            P("fsdp", None),
            P("fsdp"),
            P("fsdp"),
            P("fsdp"),
        ),
        check_vma=False,
    )
```

profile of v0, /device:TPU:14, one launch (start us, length us, event | category | flops | bytes accessed | tf_op | source)
XLA Modules:
  0.0 1032.9 jit_solution(17065472800059778839)
XLA Ops:
  9.6 31.2 %all-gather.14.cloned.1.call-done = bf16[768,768]{1,0:T(8,128)(2,1)} async-done(((bf16[192,768]{1,0:T(8,128)(2,1)}), bf16[768,768]{1,0:T(8,128)(2,1)}) %all-gather.14.cloned.1.call-update) | async-done | bytes 1179664 | tf_op jit(solution)/shard_map/all_gather | solution.py:71
  46.4 15.2 %all-reduce.20 = (bf16[768]{0:T(1024)(128)(2,1)S(1)}, bf16[768]{0:T(1024)(128)(2,1)S(1)}, bf16[768]{0:T(1024)(128)(2,1)S(1)}, bf16[768]{0:T(1024)(128)(2,1)S(1)}...) all-reduce(bf16[768]{0:T(1024)(128)(2,1)S(1)} %dynamic-update-slice, ...), channel_id=1, replica_groups=mesh['ctx'=8,'fsdp'=4] {'fsdp'}, use_global_device_ids=true, to_apply=%add | all-reduce | flops 5376 | bytes 21504
  61.6 10.7 %all-gather.12.cloned.1.call-done = bf16[768,768]{1,0:T(8,128)(2,1)} async-done(((bf16[192,768]{1,0:T(8,128)(2,1)}), bf16[768,768]{1,0:T(8,128)(2,1)}) %all-gather.12.cloned.1.call-update) | async-done | bytes 1179664 | tf_op jit(solution)/shard_map/all_gather | solution.py:72
  78.8 12.2 %all-gather.2 = bf16[4,1,768]{2,1,0:T(2,128)(2,1)S(1)} all-gather(bf16[1,1,768]{2,1,0:T(2,128)(2,1)S(1)} %reshape.543), channel_id=1, replica_groups=mesh['ctx'=8,'fsdp'=4] {'fsdp'}, dimensions={0}, use_global_device_ids=true | all-gather | bytes 7680 | tf_op jit(solution)/shard_map/all_gather | solution.py:83
  94.0 9.5 all-gather.16.cloned.1.call-done
  107.4 29.6 %all-gather.26.cloned.1.call-done = bf16[2048,768]{1,0:T(8,128)(2,1)} async-done(((bf16[256,768]{1,0:T(8,128)(2,1)}), bf16[2048,768]{1,0:T(8,128)(2,1)}) %all-gather.26.cloned.1.call-update) | async-done | bytes 3145744 | tf_op jit(solution)/shard_map/all_gather | solution.py:164
  137.0 4.7 copy.61
  141.7 54.5 %while.54 = (s32[]{:T(128)}, f32[1,12,256]{2,1,0:T(8,128)S(1)}, f32[1,12,256]{2,1,0:T(8,128)}, s32[1,256]{1,0:T(1,128)}, s32[1,2048]{1,0:T(1,128)}, /*index=5*/b...) while((s32[]{:T(128)}, f32[1,12,256]{2,1,0:T(8,128)S(1)}, ...), condition=%wide.region_3.4_spmd.clone, body=%wide.region_0.3_spmd.clone.sunk | while | flops 107035656 | bytes 8585474 | solution.py:129
  197.0 54.8 %while.55 = (s32[]{:T(128)}, f32[1,256,12,64]{1,3,2,0:T(8,128)}, bf16[1,2048,768]{2,1,0:T(8,128)(2,1)}, s32[1,256]{1,0:T(1,128)}, s32[1,2048]{1,0:T(1,128)}, /*i...) while((s32[]{:T(128)}, f32[1,256,12,64]{1,3,2,0:T(8,128)}, ...), condition=%wide.region_5.6_spmd.clone, body=%wide.region_4.5_spmd.clone.sunk | while | flops 205717504 | bytes 5259449 | solution.py:129
  255.9 36.2 %all-gather.20.cloned.1.call-done = bf16[768,3072]{1,0:T(8,128)(2,1)} async-done(((bf16[192,3072]{1,0:T(8,128)(2,1)}), bf16[768,3072]{1,0:T(8,128)(2,1)}) %all-gather.20.cloned.1.call-update) | async-done | bytes 4718608 | tf_op jit(solution)/shard_map/all_gather | solution.py:81
  292.1 11.4 %multiply_convert_fusion.1 = (bf16[256,3072]{1,0:T(8,128)(2,1)S(1)}, f32[256,3072]{1,0:T(8,128)}, f32[256,3072]{1,0:T(8,128)}) fusion(f32[3072]{0:T(1024)} %bitcast.288, bf16[768,3072]{1,0:T(8,128)(2,1)} %all-gather.20.cloned.1.call-done, f32[256,768]{1,0:T(8,128)S(1)} %get-tuple-element.938, f32[768]{0:T(1024)S(1)} %copy-done.38, f32[768]{0:T(1024)S(1)} %copy-done.37, ...), kind=kOutput, calls=%fused_computation.56 | convolution fusion | flops 1260847104 | bytes 13389824 | tf_op jit(solution)/shard_map/dot_general | solution.py:35
  303.4 78.1 %all-gather.22.cloned.1.call-done = bf16[3072,768]{1,0:T(8,128)(2,1)} async-done(((bf16[768,768]{1,0:T(8,128)(2,1)}), bf16[3072,768]{1,0:T(8,128)(2,1)}) %all-gather.22.cloned.1.call-update) | async-done | bytes 4718608 | tf_op jit(solution)/shard_map/all_gather | solution.py:82
  400.3 229.1 %while.56 = (s32[]{:T(128)}, bf16[1,256,768]{1,2,0:T(8,128)(2,1)}, bf16[1,256,768]{1,2,0:T(8,128)(2,1)S(1)}, f32[1,256,768]{1,2,0:T(8,128)}, f32[1,256,768]{1,2,...) while((s32[]{:T(128)}, bf16[1,256,768]{1,2,0:T(8,128)(2,1)}, ...), condition=%wide.region_16.17_spmd.clone, body=%wide.region_15.16_spmd.clone.sunk | while | flops 515178496 | bytes 39264880 | solution.py:280
  424.7 4.1 collective-permute-done.1
  453.2 4.1 collective-permute-done.1
  481.8 4.1 collective-permute-done.1
  510.3 4.1 collective-permute-done.1
  538.8 4.1 collective-permute-done.1
  567.3 4.1 collective-permute-done.1
  595.9 4.1 collective-permute-done.1
  625.3 4.1 collective-permute-done.1
  642.4 5.2 convolution_convert_fusion.1
  649.0 4.6 convolution_convert_fusion
  653.7 14.3 %reduce-scatter.19.cloned.1.call-done = bf16[192,768]{1,0:T(8,128)(2,1)} async-done(((bf16[768,768]{1,0:T(8,128)(2,1)}), bf16[192,768]{1,0:T(8,128)(2,1)}) %reduce-scatter.19.cloned.1.call-update) | async-done | bytes 294928
  669.9 28.2 %reduce-scatter.21.cloned.1.call-done = bf16[192,768]{1,0:T(8,128)(2,1)} async-done(((bf16[768,768]{1,0:T(8,128)(2,1)}), bf16[192,768]{1,0:T(8,128)(2,1)}) %reduce-scatter.21.cloned.1.call-update) | async-done | bytes 294928
  699.9 28.4 %reduce-scatter.23.cloned.1.call-done = bf16[192,768]{1,0:T(8,128)(2,1)} async-done(((bf16[768,768]{1,0:T(8,128)(2,1)}), bf16[192,768]{1,0:T(8,128)(2,1)}) %reduce-scatter.23.cloned.1.call-update) | async-done | bytes 294928
  730.2 28.2 %reduce-scatter.13.cloned.1.call-done = bf16[192,768]{1,0:T(8,128)(2,1)} async-done(((bf16[768,768]{1,0:T(8,128)(2,1)}), bf16[192,768]{1,0:T(8,128)(2,1)}) %reduce-scatter.13.cloned.1.call-update) | async-done | bytes 294928 | tf_op jit(solution)/shard_map/reduce_scatter | solution.py:315
  758.4 88.3 %reduce-scatter.15.cloned.1.call-done = bf16[192,3072]{1,0:T(8,128)(2,1)} async-done(((bf16[768,3072]{1,0:T(8,128)(2,1)}), bf16[192,3072]{1,0:T(8,128)(2,1)}) %reduce-scatter.15.cloned.1.call-update) | async-done | bytes 1179664 | tf_op jit(solution)/shard_map/reduce_scatter | solution.py:327
  846.7 88.0 %reduce-scatter.17.cloned.1.call-done = bf16[768,768]{1,0:T(8,128)(2,1)} async-done(((bf16[3072,768]{1,0:T(8,128)(2,1)}), bf16[768,768]{1,0:T(8,128)(2,1)}) %reduce-scatter.17.cloned.1.call-update) | async-done | bytes 1179664 | tf_op jit(solution)/shard_map/reduce_scatter | solution.py:333
  936.7 14.9 %all-reduce.19 = (bf16[768]{0:T(1024)(128)(2,1)S(1)}, bf16[768]{0:T(1024)(128)(2,1)S(1)}, bf16[768]{0:T(1024)(128)(2,1)S(1)}, bf16[768]{0:T(1024)(128)(2,1)S(1)}...) all-reduce(bf16[768]{0:T(1024)(128)(2,1)S(1)} %dynamic-update-slice, ...), channel_id=1, replica_groups=mesh['ctx'=8,'fsdp'=4] {'fsdp'}, use_global_device_ids=true, to_apply=%add.7 | all-reduce | flops 9984 | bytes 39936
  952.3 12.1 %all-reduce.17 = (bf16[192]{0:T(256)(128)(2,1)S(1)}, bf16[192]{0:T(256)(128)(2,1)S(1)}, bf16[192]{0:T(256)(128)(2,1)S(1)}, bf16[192]{0:T(256)(128)(2,1)S(1)}, bf...) all-reduce(bf16[192]{0:T(256)(128)(2,1)S(1)} %dynamic-slice.9, ...), channel_id=1, replica_groups=mesh['ctx'=8,'fsdp'=4] {'ctx'}, use_global_device_ids=true, to_apply=%region_21.22 | all-reduce | flops 2304 | bytes 9216 | tf_op jit(solution)/shard_map/psum | solution.py:347
  975.9 42.1 %all-reduce.23.cloned.1.call-done = (bf16[192,768]{0,1:T(8,128)(2,1)}, bf16[192,768]{0,1:T(8,128)(2,1)}, bf16[192,768]{0,1:T(8,128)(2,1)}, bf16[192,768]{1,0:T(8...) async-done(((bf16[192,768]{0,1:T(8,128)(2,1)}, bf16[192,768]{0,1:T(8,128)(2,1)}, bf16[192,768]{0,1:T(8,128)(2,1)}, bf16[192,768]{1,0:T(8,128)(2,1)}, ...) | async-done | bytes 3538960 | tf_op jit(solution)/shard_map/psum | solution.py:347
  (658 shorter events, 389.3 us)
Async XLA Ops:
  7.3 33.5 %all-gather.14.cloned.1.call-start = ((), (), s32[]{:S(2)}) async-start(), calls=%async_computation.7 | async-start | bytes 1474560 | tf_op jit(solution)/shard_map/all_gather | solution.py:71
  8.0 64.2 %all-gather.12.cloned.1.call-start = ((), (), s32[]{:S(2)}) async-start(), calls=%async_computation.6 | async-start | bytes 1474560 | tf_op jit(solution)/shard_map/all_gather | solution.py:72
  8.8 94.8 %all-gather.16.cloned.1.call-start = ((), (), s32[]{:S(2)}) async-start(), calls=%async_computation.8 | async-start | bytes 1474560 | tf_op jit(solution)/shard_map/all_gather | solution.py:70
  9.5 127.5 %all-gather.26.cloned.1.call-start = ((), (), s32[]{:S(2)}) async-start(), calls=%async_computation.16 | async-start | bytes 3538944 | tf_op jit(solution)/shard_map/all_gather | solution.py:164
  43.4 153.5 %all-gather.24.cloned.1.call-start = ((), (), s32[]{:S(2)}) async-start(), calls=%async_computation.15 | async-start | bytes 3538944 | tf_op jit(solution)/shard_map/all_gather | solution.py:165
  74.8 178.8 %all-gather.18.cloned.1.call-start = ((), (), s32[]{:S(2)}) async-start(), calls=%async_computation.9 | async-start | bytes 1474560 | tf_op jit(solution)/shard_map/all_gather | solution.py:73
  75.4 216.7 %all-gather.20.cloned.1.call-start = ((), (), s32[]{:S(2)}) async-start(), calls=%async_computation.10 | async-start | bytes 5898240 | tf_op jit(solution)/shard_map/all_gather | solution.py:81
  76.1 305.4 %all-gather.22.cloned.1.call-start = ((), (), s32[]{:S(2)}) async-start(), calls=%async_computation.11 | async-start | bytes 5898240 | tf_op jit(solution)/shard_map/all_gather | solution.py:82
  76.9 591.1 %reduce-scatter.19.cloned.1.call-start = ((), (), s32[]{:S(2)}) async-start(), calls=%async_computation.17 | async-start | bytes 1474560
  410.5 10.0 collective-permute-start.3
  411.0 13.8 %collective-permute-start = (bf16[1,256,768]{1,2,0:T(8,128)(2,1)S(1)}, bf16[1,256,768]{1,2,0:T(8,128)(2,1)}, u32[]{:S(2)}, u32[]{:S(2)}) collective-permute-start(bf16[1,256,768]{1,2,0:T(8,128)(2,1)S(1)} %copy.108), channel_id=1, source_target_pairs={{28,0},{0,4},{4,8},{8,12},{12,16},{16,20},{20,24},{24,28},{29,1},{... | collective-permute-start | bytes 1179656 | tf_op jit(solution)/shard_map/while/body/eval_jaxpr/ppermute | solution.py:17
  411.0 17.9 %collective-permute-start.1 = (bf16[1,256,768]{1,2,0:T(8,128)(2,1)}, bf16[1,256,768]{1,2,0:T(8,128)(2,1)S(1)}, u32[]{:S(2)}, u32[]{:S(2)}) collective-permute-start(bf16[1,256,768]{1,2,0:T(8,128)(2,1)} %copy.109), channel_id=1, source_target_pairs={{28,0},{0,4},{4,8},{8,12},{12,16},{16,20},{20,24},{24,28},{29,1},{... | collective-permute-start | bytes 1179656 | tf_op jit(solution)/shard_map/while/body/eval_jaxpr/ppermute | solution.py:17
  440.4 12.9 %collective-permute-start = (bf16[1,256,768]{1,2,0:T(8,128)(2,1)S(1)}, bf16[1,256,768]{1,2,0:T(8,128)(2,1)}, u32[]{:S(2)}, u32[]{:S(2)}) collective-permute-start(bf16[1,256,768]{1,2,0:T(8,128)(2,1)S(1)} %copy.108), channel_id=1, source_target_pairs={{28,0},{0,4},{4,8},{8,12},{12,16},{16,20},{20,24},{24,28},{29,1},{... | collective-permute-start | bytes 1179656 | tf_op jit(solution)/shard_map/while/body/eval_jaxpr/ppermute | solution.py:17
  440.4 17.0 %collective-permute-start.1 = (bf16[1,256,768]{1,2,0:T(8,128)(2,1)}, bf16[1,256,768]{1,2,0:T(8,128)(2,1)S(1)}, u32[]{:S(2)}, u32[]{:S(2)}) collective-permute-start(bf16[1,256,768]{1,2,0:T(8,128)(2,1)} %copy.109), channel_id=1, source_target_pairs={{28,0},{0,4},{4,8},{8,12},{12,16},{16,20},{20,24},{24,28},{29,1},{... | collective-permute-start | bytes 1179656 | tf_op jit(solution)/shard_map/while/body/eval_jaxpr/ppermute | solution.py:17
  469.8 12.0 %collective-permute-start = (bf16[1,256,768]{1,2,0:T(8,128)(2,1)S(1)}, bf16[1,256,768]{1,2,0:T(8,128)(2,1)}, u32[]{:S(2)}, u32[]{:S(2)}) collective-permute-start(bf16[1,256,768]{1,2,0:T(8,128)(2,1)S(1)} %copy.108), channel_id=1, source_target_pairs={{28,0},{0,4},{4,8},{8,12},{12,16},{16,20},{20,24},{24,28},{29,1},{... | collective-permute-start | bytes 1179656 | tf_op jit(solution)/shard_map/while/body/eval_jaxpr/ppermute | solution.py:17
  469.8 16.1 %collective-permute-start.1 = (bf16[1,256,768]{1,2,0:T(8,128)(2,1)}, bf16[1,256,768]{1,2,0:T(8,128)(2,1)S(1)}, u32[]{:S(2)}, u32[]{:S(2)}) collective-permute-start(bf16[1,256,768]{1,2,0:T(8,128)(2,1)} %copy.109), channel_id=1, source_target_pairs={{28,0},{0,4},{4,8},{8,12},{12,16},{16,20},{20,24},{24,28},{29,1},{... | collective-permute-start | bytes 1179656 | tf_op jit(solution)/shard_map/while/body/eval_jaxpr/ppermute | solution.py:17
  496.1 10.0 collective-permute-start.3
  499.2 11.1 %collective-permute-start = (bf16[1,256,768]{1,2,0:T(8,128)(2,1)S(1)}, bf16[1,256,768]{1,2,0:T(8,128)(2,1)}, u32[]{:S(2)}, u32[]{:S(2)}) collective-permute-start(bf16[1,256,768]{1,2,0:T(8,128)(2,1)S(1)} %copy.108), channel_id=1, source_target_pairs={{28,0},{0,4},{4,8},{8,12},{12,16},{16,20},{20,24},{24,28},{29,1},{... | collective-permute-start | bytes 1179656 | tf_op jit(solution)/shard_map/while/body/eval_jaxpr/ppermute | solution.py:17
  499.2 15.2 %collective-permute-start.1 = (bf16[1,256,768]{1,2,0:T(8,128)(2,1)}, bf16[1,256,768]{1,2,0:T(8,128)(2,1)S(1)}, u32[]{:S(2)}, u32[]{:S(2)}) collective-permute-start(bf16[1,256,768]{1,2,0:T(8,128)(2,1)} %copy.109), channel_id=1, source_target_pairs={{28,0},{0,4},{4,8},{8,12},{12,16},{16,20},{20,24},{24,28},{29,1},{... | collective-permute-start | bytes 1179656 | tf_op jit(solution)/shard_map/while/body/eval_jaxpr/ppermute | solution.py:17
  528.6 10.2 collective-permute-start
  528.6 14.3 %collective-permute-start.1 = (bf16[1,256,768]{1,2,0:T(8,128)(2,1)}, bf16[1,256,768]{1,2,0:T(8,128)(2,1)S(1)}, u32[]{:S(2)}, u32[]{:S(2)}) collective-permute-start(bf16[1,256,768]{1,2,0:T(8,128)(2,1)} %copy.109), channel_id=1, source_target_pairs={{28,0},{0,4},{4,8},{8,12},{12,16},{16,20},{20,24},{24,28},{29,1},{... | collective-permute-start | bytes 1179656 | tf_op jit(solution)/shard_map/while/body/eval_jaxpr/ppermute | solution.py:17
  558.0 13.4 %collective-permute-start.1 = (bf16[1,256,768]{1,2,0:T(8,128)(2,1)}, bf16[1,256,768]{1,2,0:T(8,128)(2,1)S(1)}, u32[]{:S(2)}, u32[]{:S(2)}) collective-permute-start(bf16[1,256,768]{1,2,0:T(8,128)(2,1)} %copy.109), channel_id=1, source_target_pairs={{28,0},{0,4},{4,8},{8,12},{12,16},{16,20},{20,24},{24,28},{29,1},{... | collective-permute-start | bytes 1179656 | tf_op jit(solution)/shard_map/while/body/eval_jaxpr/ppermute | solution.py:17
  579.8 10.3 collective-permute-start.2
  587.4 12.6 %collective-permute-start.1 = (bf16[1,256,768]{1,2,0:T(8,128)(2,1)}, bf16[1,256,768]{1,2,0:T(8,128)(2,1)S(1)}, u32[]{:S(2)}, u32[]{:S(2)}) collective-permute-start(bf16[1,256,768]{1,2,0:T(8,128)(2,1)} %copy.109), channel_id=1, source_target_pairs={{28,0},{0,4},{4,8},{8,12},{12,16},{16,20},{20,24},{24,28},{29,1},{... | collective-permute-start | bytes 1179656 | tf_op jit(solution)/shard_map/while/body/eval_jaxpr/ppermute | solution.py:17
  608.4 11.1 %collective-permute-start.2 = (bf16[1,256,768]{1,2,0:T(8,128)(2,1)}, bf16[1,256,768]{1,2,0:T(8,128)(2,1)}, u32[]{:S(2)}, u32[]{:S(2)}) collective-permute-start(bf16[1,256,768]{1,2,0:T(8,128)(2,1)} %fusion.149), channel_id=1, source_target_pairs={{28,0},{0,4},{4,8},{8,12},{12,16},{16,20},{20,24},{24,28},{29,1},{... | collective-permute-start | bytes 1179656 | tf_op jit(solution)/shard_map/while/body/eval_jaxpr/ppermute | solution.py:17
  616.8 12.6 %collective-permute-start.1 = (bf16[1,256,768]{1,2,0:T(8,128)(2,1)}, bf16[1,256,768]{1,2,0:T(8,128)(2,1)S(1)}, u32[]{:S(2)}, u32[]{:S(2)}) collective-permute-start(bf16[1,256,768]{1,2,0:T(8,128)(2,1)} %copy.109), channel_id=1, source_target_pairs={{28,0},{0,4},{4,8},{8,12},{12,16},{16,20},{20,24},{24,28},{29,1},{... | collective-permute-start | bytes 1179656 | tf_op jit(solution)/shard_map/while/body/eval_jaxpr/ppermute | solution.py:17
  634.4 63.7 %reduce-scatter.21.cloned.1.call-start = ((), (), s32[]{:S(2)}) async-start(), calls=%async_computation.18 | async-start | bytes 1474560
  636.4 91.9 %reduce-scatter.23.cloned.1.call-start = ((), (), s32[]{:S(2)}) async-start(), calls=%async_computation.19 | async-start | bytes 1474560
  640.7 117.7 %reduce-scatter.13.cloned.1.call-start = ((), (), s32[]{:S(2)}) async-start(), calls=%async_computation.12 | async-start | bytes 1474560 | tf_op jit(solution)/shard_map/reduce_scatter | solution.py:315
  642.3 204.4 %reduce-scatter.15.cloned.1.call-start = ((), (), s32[]{:S(2)}) async-start(), calls=%async_computation.13 | async-start | bytes 5898240 | tf_op jit(solution)/shard_map/reduce_scatter | solution.py:327
  647.6 287.0 %reduce-scatter.17.cloned.1.call-start = ((), (), s32[]{:S(2)}) async-start(), calls=%async_computation.14 | async-start | bytes 5898240 | tf_op jit(solution)/shard_map/reduce_scatter | solution.py:333
  653.7 364.2 %all-reduce.23.cloned.1.call-start = ((), (), s32[]{:S(2)}) async-start(), calls=%async_computation.20 | async-start | bytes 7667712 | tf_op jit(solution)/shard_map/psum | solution.py:347
  (138 other events, 4699.2 us)
Sparse Core Ops, SparseCore 0:
  9.7 31.0 all-gather.13
  42.3 29.8 all-gather.11
  73.8 29.7 all-gather.15
  105.9 31.0 all-gather.25
  139.3 32.3 all-gather.23
  173.0 30.8 all-gather.17
  205.5 86.4 all-gather.19
  293.6 87.8 all-gather.21
  634.5 33.4 reduce-scatter.18
  670.1 27.8 reduce-scatter.20
  700.4 27.8 reduce-scatter.22
  730.5 27.8 reduce-scatter.12
  760.7 85.9 reduce-scatter.14
  848.8 85.7 reduce-scatter.16
  939.2 78.6 all-reduce.22
where the time goes:
time: 1040 us; the launch traced here: 1030 us
  waiting for transfers between devices  588 us (57%)
  matrix products  142 us (14%)
  other arithmetic  101 us (10%)
  local copies, waits for them, and re-layouts  97.8 us (9%)
  blocking collectives  54.4 us (5%)
  starting transfers between devices  32.3 us (3%)
  between operations  16.7 us (2%)
    reduce_scatter x1, waiting for transfers between devices, per_device(): lax.psum_scatter(grad_w_inner.astype(jnp.bfloat16), 'fsdp', scatter_dimen...  88.3 us
    reduce_scatter x1, waiting for transfers between devices, per_device(): lax.psum_scatter(grad_w_outer.astype(jnp.bfloat16), 'fsdp', scatter_dimen...  88 us
    all_gather x1, waiting for transfers between devices, per_device(): lax.all_gather(w_outer, 'fsdp', axis=0, tiled=True)  78.1 us
    unnamed x18, waiting for transfers between devices  74.9 us
    ppermute x32, waiting for transfers between devices, from_behind(): return lax.ppermute(block, axis, route)  71.3 us
    psum x1, waiting for transfers between devices, per_device(): lax.psum(shortened(tuple(shards)), 'ctx')  42.1 us
    all_gather x1, waiting for transfers between devices, per_device(): lax.all_gather(w_inner, 'fsdp', axis=0, tiled=True)  36.2 us
    ppermute x32, starting transfers between devices, from_behind(): return lax.ppermute(block, axis, route)  31.4 us
  transfers between devices with their start and end apart: 47, of which 38 were waited for; matrix products, arithmetic and copies ran while one was open for 23% of the time, Pallas kernels for 0%

commit v1 on v0

v1 whole, which is shorter than its diff:
```python
import functools
import math

import jax
import jax.numpy as jnp
from jax import lax
from jax.experimental import pallas as pl
from jax.experimental.pallas import tpu as pltpu
from jax.sharding import PartitionSpec as P

HEADS = 12
GROUPS = 4
LN_EPS = 1e-12
MASKED = -1e30
f32 = jnp.float32
b16 = jnp.bfloat16


def swap(x, axis, flip):
    return lax.ppermute(x, axis, [(i, i ^ flip) for i in range(lax.axis_size(axis))])


def pick(x, index):
    return lax.dynamic_index_in_dim(x, index, 0, keepdims=False)


def nn(a, b):
    return lax.dot_general(a, b, (((1,), (0,)), ((), ())), preferred_element_type=f32)


def nt(a, b):
    return lax.dot_general(a, b, (((1,), (1,)), ((), ())), preferred_element_type=f32)


def tn(a, b):
    return lax.dot_general(a, b, (((0,), (0,)), ((), ())), preferred_element_type=f32)


def whole_call(body, outs, n_in, scratch=(), name=None):
    specs = [pl.BlockSpec(memory_space=pltpu.SMEM)]
    specs += [pl.BlockSpec(memory_space=pltpu.VMEM)] * (n_in - 1)
    return pl.pallas_call(
        body,
        out_shape=outs,
        in_specs=specs,
        out_specs=[pl.BlockSpec(memory_space=pltpu.VMEM)] * len(outs),
        scratch_shapes=list(scratch),
        name=name,
    )


def shape(dims, dtype):
    return jax.ShapeDtypeStruct(dims, dtype)


def row_sum(x):
    return jnp.sum(x, axis=0, keepdims=True)


def normalised(x):
    center = x - jnp.mean(x, axis=-1, keepdims=True)
    spread = jnp.mean(center * center, axis=-1, keepdims=True)
    rate = lax.rsqrt(spread + LN_EPS)
    return center * rate, rate


def norm_back(u, hat, rate):
    along = jnp.mean(u * hat, axis=-1, keepdims=True)
    return rate * (u - jnp.mean(u, axis=-1, keepdims=True) - hat * along)


def project_kernel(sc, t0, t1, t2, t3, own, par, shift, q_out, kv_out, w_out):
    z, c = sc[0], sc[1]
    ranks, half = own.shape[0], own.shape[1]
    width = q_out.shape[-1]
    for a in range(ranks):
        base = (z ^ a) * (2 * half)
        w_out[pl.ds(pl.multiple_of(base + c * half, 16), half), :] = own[a]
        w_out[pl.ds(pl.multiple_of(base + (1 - c) * half, 16), half), :] = par[a]
    for s, t in enumerate((t0, t1, t2, t3)):
        y = nn(t[...], w_out[...]) + shift[...]
        q_out[s] = y[:, :width].astype(b16)
        kv_out[s] = y[:, width:].astype(b16)


def project_back_kernel(sc, t0, t1, t2, t3, dq, dkv, dkv_in, w, dx_own, dx_send, gw, gb):
    width = dq.shape[-1]
    grads = []
    for s in range(GROUPS):
        right = (dkv[s] + dkv_in[s].astype(f32)).astype(b16)
        grads.append(jnp.concatenate([dq[s], right], axis=1))
    dx_own[...] = nt(grads[0], w[...])
    for s in range(1, GROUPS):
        dx_send[s - 1] = nt(grads[s], w[...]).astype(b16)
    total = tn(t0[...], grads[0])
    sums = row_sum(grads[0].astype(f32))
    for s, t in ((1, t1), (2, t2), (3, t3)):
        total += tn(t[...], grads[s])
        sums += row_sum(grads[s].astype(f32))
    gw[...] = total.astype(b16)
    gb[...] = sums


def block_of(sc, entry, s):
    rank = sc[2] ^ entry
    return ((rank >> 1) * GROUPS + (sc[3] ^ s)) * 2 + (rank & 1)


def gather_blocks(sc, parts, kv_all):
    @pl.when(pl.program_id(0) == 0)
    def _():
        for entry, part in enumerate(parts):
            for s in range(GROUPS):
                kv_all[block_of(sc, entry, s)] = part[s]


def attend_kernel(sc, span, q, seg_rows, seg_cols, *rest):
    parts, (mixed, low_out, log_out), (kv_all, kept) = rest[:-5], rest[-5:-2], rest[-2:]
    gather_blocks(sc, parts, kv_all)
    here = block_of(sc, 0, pl.program_id(0))
    low, high = span[here, 0], span[here, 1]
    rows = q.shape[1]
    per_group = q.shape[2] // 128
    seg_q = seg_rows[here]
    left = lax.broadcasted_iota(jnp.int32, (rows, 128), 1) < 64
    one = jnp.ones((rows, 128), b16)
    log_out[...] = jnp.zeros(log_out.shape, f32)
    for h in range(per_group):
        lanes = slice(h * 128, (h + 1) * 128)
        qh = q[0, :, lanes]

        def first(j, top, lanes=lanes, qh=qh):
            st = nt(kv_all[j, :, lanes], qh)
            seg = seg_cols[j]
            for w in range(0, rows, 128):
                ok = seg == seg_q[:, w : w + 128]
                kept[j, :, w : w + 128] = jnp.where(ok, st[:, w : w + 128], MASKED)
            return jnp.maximum(top, jnp.max(kept[j], axis=0, keepdims=True))

        top = lax.fori_loop(low, high, first, jnp.full((1, rows), MASKED, f32))

        def second(j, state, lanes=lanes, top=top):
            total, acc = state
            pt = jnp.exp(kept[j] - top)
            values = jnp.where(left, one, kv_all[j, :, lanes])
            return total + row_sum(pt), acc + tn(pt.astype(b16), values)

        total, acc = lax.fori_loop(
            low, high, second, (jnp.zeros((1, rows), f32), jnp.zeros((rows, 128), f32))
        )
        out = acc[:, 64:] / acc[:, :64]
        mixed[0, :, h * 64 : (h + 1) * 64] = out
        low_out[0, :, h * 64 : (h + 1) * 64] = out.astype(b16)
        log_out[0, h : h + 1, :] = top + jnp.log(total)


def attend_back_kernel(sc, span, q, seg_rows, seg_cols, grad, mixed, logs, *rest):
    count = (len(rest) - 4) // 2
    parts = rest[:count]
    dq, dkv_own = rest[count], rest[count + 1]
    dkv_send = rest[count + 2 : 2 * count + 1]
    kv_all, dkv_all, dq_acc = rest[2 * count + 1 :]
    step = pl.program_id(0)
    gather_blocks(sc, parts, kv_all)

    @pl.when(step == 0)
    def _():
        dkv_all[...] = jnp.zeros(dkv_all.shape, f32)

    here = block_of(sc, 0, step)
    low, high = span[here, 0], span[here, 1]
    rows = q.shape[1]
    per_group = q.shape[2] // 128
    seg_q = seg_rows[here]
    gap = jnp.zeros((rows, 64), b16)
    for h in range(per_group):
        lanes = slice(h * 128, (h + 1) * 128)
        part = slice(h * 64, (h + 1) * 64)
        qh = q[0, :, lanes]
        gh = grad[0, :, part]
        along = jnp.sum(gh.astype(f32) * mixed[0, :, part], axis=1, keepdims=True)
        balance = jnp.transpose(jnp.broadcast_to(along, (rows, 128)))[0:1]
        gh = jnp.concatenate([gap, gh], axis=1)
        log_row = logs[0, h : h + 1, :]
        dq_acc[...] = jnp.zeros(dq_acc.shape, f32)
        both = jnp.concatenate([qh, gh], axis=0)

        @pl.loop(low, high)
        def _(j, lanes=lanes, qh=qh, gh=gh, balance=balance, log_row=log_row, both=both):
            kv = kv_all[j, :, lanes]
            seg = seg_cols[j]
            ok = jnp.concatenate([seg == seg_q[:, w : w + 128] for w in range(0, rows, 128)], axis=1)
            st = jnp.where(ok, nt(kv, qh), MASKED)
            pt = jnp.exp(st - log_row)
            dst = (pt * (nt(kv, gh) - balance)).astype(b16)
            dkv_all[j, :, lanes] += nn(jnp.concatenate([dst, pt.astype(b16)], axis=1), both)
            dq_acc[...] += tn(dst, kv)

        keep = lax.broadcasted_iota(jnp.int32, (rows, 128), 1) < 64
        dq[0, :, lanes] = jnp.where(keep, dq_acc[...], 0.0).astype(b16)

    @pl.when(step == pl.num_programs(0) - 1)
    def _():
        for s in range(GROUPS):
            dkv_own[s] = dkv_all[block_of(sc, 0, s)]
            for entry, send in enumerate(dkv_send):
                send[s] = dkv_all[block_of(sc, entry + 1, s)].astype(b16)


def lay_out(sc, pieces, own, par):
    z, c = sc[0], sc[1]
    ranks, rows = own.shape[0], own.shape[1]
    for a in range(ranks):
        at = pl.ds(pl.multiple_of((z ^ a) * rows, 16), rows)
        pieces[c, at, :] = own[a]
        pieces[1 - c, at, :] = par[a]


def group_rows(sc, s, size):
    return pl.ds(pl.multiple_of((sc[3] ^ s) * size, 16), size)


def out_kernel(sc, tok, a0, a1, a2, a3, own, par, shift, gain, bias, hat, rate, low, w):
    lay_out(sc, w, own, par)
    size = a0.shape[1]
    half = w.shape[2]
    sides = []
    for side in range(2):
        y = tok[:, side * half : (side + 1) * half].astype(f32)
        for s, a in enumerate((a0, a1, a2, a3)):
            y += nn(a[...], w[side, group_rows(sc, s, size), :])
        sides.append(y)
    resid = jnp.concatenate(sides, axis=1) + shift[...]
    h, r = normalised(resid)
    hat[...] = h
    rate[...] = jnp.broadcast_to(r, rate.shape)
    low[...] = (h * gain[...] + bias[...]).astype(b16)


def weights_of(sc, pieces, w):
    z = sc[0]
    rows = pieces.shape[1]
    for a in range(pieces.shape[0]):
        w[pl.ds(pl.multiple_of((z ^ a) * rows, 16), rows), :] = pieces[a]


def feed_kernel(sc, n_own, n_par, i0, i1, i2, i3, o0, o1, o2, o3, shift, act, slope, y_own, y_par, wi, wo):
    rows = n_own.shape[0]
    tokens = jnp.concatenate([n_own[...], n_par[...]], axis=0)
    total = jnp.zeros((2 * rows, n_own.shape[1]), f32)
    for s, (i, o) in enumerate(((i0, o0), (i1, o1), (i2, o2), (i3, o3))):
        weights_of(sc, i, wi.at[s])
        weights_of(sc, o, wo.at[s])
        inner = nn(tokens, wi[s]) + shift[s : s + 1, :]
        phi = 0.5 * (1.0 + lax.erf(inner * math.sqrt(0.5)))
        dens = jnp.exp(-0.5 * inner * inner) * (1.0 / math.sqrt(2.0 * math.pi))
        a = (inner * phi).astype(b16)
        act[s] = a
        slope[s] = (phi + inner * dens).astype(slope.dtype)
        total += nn(a, wo[s])
    y_own[...] = total[:rows]
    y_par[...] = total[rows:]


def close_kernel(sc, hat1, gain1, bias1, y_own, y_par, shift, gain, bias, cot, result, grad_two, low, sums):
    normed = hat1[...] * gain1[...] + bias1[...]
    h, r = normalised(normed + y_own[...] + y_par[...] + shift[...])
    result[...] = (h * gain[...] + bias[...]).astype(b16)
    c = cot[...].astype(f32)
    g = norm_back(c * gain[...], h, r)
    grad_two[...] = g
    g_low = g.astype(b16)
    low[...] = g_low
    sums[...] = jnp.zeros(sums.shape, f32)
    sums[0:1, :] = row_sum(g_low.astype(f32))
    sums[1:2, :] = row_sum(c * h)
    sums[2:3, :] = row_sum(c)


def feed_back_kernel(sc, g_own, g_par, i0, i1, i2, i3, o0, o1, o2, o3, slope, gi_out, y_own, y_par, gb, wi, wo):
    rows = g_own.shape[0]
    grads = jnp.concatenate([g_own[...], g_par[...]], axis=0)
    total = jnp.zeros((2 * rows, g_own.shape[1]), f32)
    for s, (i, o) in enumerate(((i0, o0), (i1, o1), (i2, o2), (i3, o3))):
        weights_of(sc, i, wi.at[s])
        weights_of(sc, o, wo.at[s])
        gi = (nt(grads, wo[s]) * slope[s].astype(f32)).astype(b16)
        gi_out[s] = gi
        gb[s : s + 1, :] = row_sum(gi.astype(f32))
        total += nt(gi, wi[s])
    y_own[...] = total[:rows]
    y_par[...] = total[rows:]


def feed_weights_kernel(sc, n_own, n_par, g_own, g_par, act, gi, wi0, wi1, wi2, wi3, wo0, wo1, wo2, wo3):
    tokens = jnp.concatenate([n_own[...], n_par[...]], axis=0)
    grads = jnp.concatenate([g_own[...], g_par[...]], axis=0)
    for s, (i, o) in enumerate(((wi0, wo0), (wi1, wo1), (wi2, wo2), (wi3, wo3))):
        i[...] = tn(tokens, gi[s]).astype(b16)
        o[...] = tn(act[s], grads).astype(b16)


def first_back_kernel(sc, grad_two, y_own, y_par, hat, rate, gain, own, par, a0, a1, a2, a3,
                      grad_one, b0, b1, b2, b3, gw_own, gw_par, sums, w):
    lay_out(sc, w, own, par)
    c = sc[1]
    gn = grad_two[...] + y_own[...] + y_par[...]
    h = hat[...]
    g = norm_back(gn * gain[...], h, rate[:, 0:1])
    grad_one[...] = g
    g_low = g.astype(b16)
    sums[...] = jnp.zeros(sums.shape, f32)
    sums[0:1, :] = row_sum(g_low.astype(f32))
    sums[1:2, :] = row_sum(gn * h)
    sums[2:3, :] = row_sum(gn)
    half = w.shape[2]
    lo, hi = g_low[:, :half], g_low[:, half:]
    mine = jnp.where(c == 0, lo, hi)
    other = jnp.where(c == 0, hi, lo)
    for s, (a, b) in enumerate(((a0, b0), (a1, b1), (a2, b2), (a3, b3))):
        at = group_rows(sc, s, b.shape[1])
        b[...] = (nt(lo, w[0, at, :]) + nt(hi, w[1, at, :])).astype(b16)
        gw_own[at, :] = tn(a[...], mine)
        gw_par[at, :] = tn(a[...], other).astype(b16)


def per_device(
    tokens,
    segments,
    w_query,
    b_query,
    w_key,
    w_value,
    b_value,
    w_out,
    b_out,
    gain_attention,
    bias_attention,
    w_inner,
    b_inner,
    w_outer,
    b_outer,
    gain_feed,
    bias_feed,
    cotangent,
):
    n = lax.axis_size("ctx")
    ranks = lax.axis_size("fsdp")
    place = lax.axis_index("ctx")
    z = lax.axis_index("fsdp")
    rows, d = tokens.shape[1], tokens.shape[2]
    ff = w_inner.shape[1]
    c, chip = place & 1, place >> 1
    g, r = chip % GROUPS, chip // GROUPS
    sets = n // GROUPS
    rank = r * 2 + c
    per_group = HEADS // GROUPS
    hd = d // HEADS
    gw = per_group * hd
    dz, fz = d // ranks, ff // ranks
    half = dz // 2
    piece = fz // (2 * GROUPS)
    wide = per_group * 2 * hd
    sc = jnp.stack([z, c, rank, g]).astype(jnp.int32)

    def over_z(x):
        return [x] + [swap(x, "fsdp", a) for a in range(1, ranks)]

    def over_group(x):
        return [x] + [swap(x, "ctx", s << 1) for s in range(1, GROUPS)]

    def over_sets(x):
        flips = [(t & 1) | ((t >> 1) * 2 * GROUPS) for t in range(sets)]
        return [x if f == 0 else swap(x, "ctx", f) for f in flips]

    tok = tokens[0]
    toks = over_group(tok)

    def head_columns(w):
        return lax.dynamic_slice_in_dim(w, g * gw, gw, 1).reshape(dz, per_group, hd)

    wq = head_columns(w_query) * jnp.asarray(0.125, b16)
    packed = jnp.concatenate(
        [
            jnp.concatenate([wq, jnp.zeros_like(wq)], axis=2).reshape(dz, wide),
            jnp.concatenate([head_columns(w_key), head_columns(w_value)], axis=2).reshape(dz, wide),
        ],
        axis=1,
    )
    vectors = jnp.concatenate(
        [b_query, b_value, b_out, gain_attention, bias_attention, b_outer, gain_feed, bias_feed, b_inner]
    )
    nvec = vectors.shape[0]
    vrows = -(-nvec // d)
    extra = -(-vrows // 8) * 8
    vec_rows = jnp.pad(vectors, (0, extra * d - nvec)).reshape(extra, d)
    first = jnp.concatenate([lax.dynamic_slice_in_dim(packed, c * half, half, 0), vec_rows], axis=0)
    first_all = jnp.stack(over_z(first))
    proj_own = first_all[:, :half]
    proj_par = swap(proj_own, "ctx", 1)
    order = z ^ jnp.arange(ranks)
    vec_all = jnp.take(first_all[:, half:].reshape(ranks, extra * d), order, axis=0)[:, :nvec].astype(f32)
    vec = [vec_all[:, k * dz : (k + 1) * dz].reshape(1, d) for k in range(8)]
    v_query, v_value, v_out, v_gain1, v_bias1, v_outer, v_gain2, v_bias2 = vec
    v_inner = vec_all[:, 8 * dz :].reshape(ranks, 2 * GROUPS, piece)

    own_piece = c * GROUPS + g
    wi = lax.dynamic_slice_in_dim(w_inner.reshape(dz, ranks, fz), own_piece * piece, piece, 2)
    wi_z = jnp.stack(over_z(wi.reshape(dz, ranks * piece)))
    wo_z = jnp.stack(over_z(lax.dynamic_slice_in_dim(w_outer, own_piece * piece, piece, 0)))
    wout_own = jnp.stack(over_z(lax.dynamic_slice_in_dim(w_out, c * (d // 2), d // 2, 1)))
    wout_par = swap(wout_own, "ctx", 1)
    wi1, wi2 = swap(wi_z, "ctx", 2), swap(wi_z, "ctx", 4)
    wi3 = swap(wi1, "ctx", 4)
    wo1, wo2 = swap(wo_z, "ctx", 2), swap(wo_z, "ctx", 4)
    wo3 = swap(wo2, "ctx", 2)
    wis, wos = (wi_z, wi1, wi2, wi3), (wo_z, wo1, wo2, wo3)
    group_order = g ^ jnp.arange(GROUPS)
    shift_inner = jnp.take(
        v_inner.transpose(1, 0, 2).reshape(2 * GROUPS, ranks * piece), c * GROUPS + group_order, axis=0
    )

    def of_group(v):
        return pick(v.reshape(GROUPS, per_group, hd), g)

    bq = of_group(v_query) * 0.125
    bv = of_group(v_value)
    zero = jnp.zeros_like(bq)
    shift_qkv = jnp.concatenate(
        [jnp.concatenate([bq, zero], axis=1).reshape(1, wide), jnp.concatenate([zero, bv], axis=1).reshape(1, wide)],
        axis=1,
    )
    q, kv, w_qkv = whole_call(
        project_kernel,
        [shape((GROUPS, rows, wide), b16), shape((GROUPS, rows, wide), b16), shape((d, 2 * wide), b16)],
        8,
        name="project",
    )(sc, *toks, proj_own, proj_par, shift_qkv)
    kvs = over_sets(kv)

    seg = segments[0].reshape(n, rows)
    begin, end = seg[:, 0], seg[:, -1]
    span = jnp.stack(
        [
            jnp.sum((end[None, :] < begin[:, None]).astype(jnp.int32), axis=1),
            jnp.sum((begin[None, :] <= end[:, None]).astype(jnp.int32), axis=1),
        ],
        axis=1,
    )
    seg_rows = seg.reshape(n, 1, rows)
    seg_cols = jnp.broadcast_to(seg[:, :, None], (n, rows, 128))

    smem = pl.BlockSpec(memory_space=pltpu.SMEM)

    def fixed(dims):
        return pl.BlockSpec(dims, lambda s: (0,) * len(dims))

    def stepped(dims):
        return pl.BlockSpec((1,) + dims, lambda s: (s,) + (0,) * len(dims))

    kv_specs = [fixed((GROUPS, rows, wide))] * sets
    mixed, att_low, logs = pl.pallas_call(
        attend_kernel,
        grid=(GROUPS,),
        in_specs=[smem, smem, stepped((rows, wide)), fixed((n, 1, rows)), fixed((n, rows, 128))] + kv_specs,
        out_specs=[stepped((rows, gw)), stepped((rows, gw)), stepped((8, rows))],
        out_shape=[
            shape((GROUPS, rows, gw), f32),
            shape((GROUPS, rows, gw), b16),
            shape((GROUPS, 8, rows), f32),
        ],
        scratch_shapes=[pltpu.VMEM((n, rows, wide), b16), pltpu.VMEM((n, rows, rows), f32)],
        name="attend",
    )(sc, span, q, seg_rows, seg_cols, *kvs)

    atts = [att_low[0]] + [swap(att_low[s], "ctx", s << 1) for s in range(1, GROUPS)]

    hat1, rate1, low = whole_call(
        out_kernel,
        [shape((rows, d), f32), shape((rows, 128), f32), shape((rows, d), b16)],
        11,
        [pltpu.VMEM((2, d, d // 2), b16)],
        name="out",
    )(sc, tok, *atts, wout_own, wout_par, v_out, v_gain1, v_bias1)
    low_par = swap(low, "ctx", 1)

    cols = ranks * piece
    scratch = [pltpu.VMEM((GROUPS, d, cols), b16), pltpu.VMEM((GROUPS, cols, d), b16)]
    act, slope, y_own, y_send = whole_call(
        feed_kernel,
        [
            shape((GROUPS, 2 * rows, cols), b16),
            shape((GROUPS, 2 * rows, cols), b16),
            shape((rows, d), f32),
            shape((rows, d), f32),
        ],
        12,
        scratch,
        name="feed",
    )(sc, low, low_par, *wis, *wos, shift_inner)
    y_par = swap(y_send, "ctx", 1)

    result, grad_two, gol, sums_two = whole_call(
        close_kernel,
        [shape((rows, d), b16), shape((rows, d), f32), shape((rows, d), b16), shape((8, d), f32)],
        10,
        name="close",
    )(sc, hat1, v_gain1, v_bias1, y_own, y_par, v_outer, v_gain2, v_bias2, cotangent[0])
    gol_par = swap(gol, "ctx", 1)

    gi, gn_own, gn_send, gb_inner = whole_call(
        feed_back_kernel,
        [
            shape((GROUPS, 2 * rows, cols), b16),
            shape((rows, d), f32),
            shape((rows, d), f32),
            shape((GROUPS, cols), f32),
        ],
        12,
        scratch,
        name="feed_back",
    )(sc, gol, gol_par, *wis, *wos, slope)
    gn_par = swap(gn_send, "ctx", 1)

    gws = whole_call(
        feed_weights_kernel,
        [shape((d, cols), b16)] * GROUPS + [shape((cols, d), b16)] * GROUPS,
        7,
        name="feed_weights",
    )(sc, low, low_par, gol, gol_par, act, gi)
    gwi, gwo = gws[:GROUPS], gws[GROUPS:]

    grad_one, *ga, gwout_own, gwout_send, sums_one = whole_call(
        first_back_kernel,
        [shape((rows, d), f32)]
        + [shape((rows, gw), b16)] * GROUPS
        + [shape((d, d // 2), f32), shape((d, d // 2), b16), shape((8, d), f32)],
        13,
        [pltpu.VMEM((2, d, d // 2), b16)],
        name="first_back",
    )(sc, grad_two, gn_own, gn_par, hat1, rate1, v_gain1, wout_own, wout_par, *atts)

    grads_att = jnp.stack([ga[0]] + [swap(ga[s], "ctx", s << 1) for s in range(1, GROUPS)])

    dq, dkv_own, *dkv_send = pl.pallas_call(
        attend_back_kernel,
        grid=(GROUPS,),
        in_specs=[smem, smem, stepped((rows, wide)), fixed((n, 1, rows)), fixed((n, rows, 128))]
        + [stepped((rows, gw)), stepped((rows, gw)), stepped((8, rows))]
        + kv_specs,
        out_specs=[stepped((rows, wide)), fixed((GROUPS, rows, wide))] + kv_specs[1:],
        out_shape=[shape((GROUPS, rows, wide), b16), shape((GROUPS, rows, wide), f32)]
        + [shape((GROUPS, rows, wide), b16)] * (sets - 1),
        scratch_shapes=[
            pltpu.VMEM((n, rows, wide), b16),
            pltpu.VMEM((n, rows, wide), f32),
            pltpu.VMEM((rows, 128), f32),
        ],
        name="attend_back",
    )(sc, span, q, seg_rows, seg_cols, grads_att, mixed, logs, *kvs)
    flips = [(t & 1) | ((t >> 1) * 2 * GROUPS) for t in range(sets)]
    dkv_in = swap(dkv_send[0], "ctx", flips[1])
    for t in range(2, sets):
        dkv_own = dkv_own + swap(dkv_send[t - 1], "ctx", flips[t]).astype(f32)

    dx_own, dx_send, gw_qkv, gb_qkv = whole_call(
        project_back_kernel,
        [
            shape((rows, d), f32),
            shape((GROUPS - 1, rows, d), b16),
            shape((d, 2 * wide), b16),
            shape((1, 2 * wide), f32),
        ],
        9,
        name="project_back",
    )(sc, *toks, dq, dkv_own, dkv_in, w_qkv)
    grad_input = grad_one + dx_own
    for s in range(1, GROUPS):
        grad_input = grad_input + swap(dx_send[s - 1], "ctx", s << 1).astype(f32)

    wi_in, wo_in = swap(gwi[3], "ctx", 2), swap(gwo[3], "ctx", 4)
    gwi2 = (gwi[2].astype(f32) + wi_in.astype(f32)).astype(b16)
    gwo1 = (gwo[1].astype(f32) + wo_in.astype(f32)).astype(b16)

    def added(first, *others):
        total = first.astype(f32)
        for other in others:
            total = total + other.astype(f32)
        return total

    swi = added(gwi[0], swap(gwi[1], "ctx", 2), swap(gwi2, "ctx", 4))
    swo = added(gwo[0], swap(gwo1, "ctx", 2), swap(gwo[2], "ctx", 4))

    def over_r(x):
        total = x
        for t in range(1, sets // 2):
            total = total + swap(x.astype(b16), "ctx", t * 2 * GROUPS).astype(f32)
        return total

    def scatter_z(x):
        low_x = x.astype(b16)
        total = pick(x, z)
        for a in range(1, ranks):
            total = total + swap(pick(low_x, z ^ a), "fsdp", a).astype(f32)
        return total.astype(b16)

    fwi = scatter_z(over_r(swi).reshape(ranks, dz, cols))
    fwo = scatter_z(over_r(swo).reshape(ranks, piece, d))
    gwout = gwout_own + swap(gwout_send, "ctx", 1).astype(f32)
    fwout = scatter_z(gwout.reshape(ranks, dz, d // 2))

    gq, gkv = gb_qkv[0, :wide].reshape(per_group, 2, hd), gb_qkv[0, wide:].reshape(per_group, 2, hd)
    mine = (jnp.arange(GROUPS) == g).astype(f32)[:, None]
    gb_query = (mine * (gq[:, 0] * 0.125).reshape(1, gw)).reshape(d)
    gb_value = (mine * gkv[:, 1].reshape(1, gw)).reshape(d)
    gbi = jnp.take(gb_inner, group_order, axis=0).reshape(GROUPS, ranks, piece).transpose(1, 0, 2)
    gbi = gbi.reshape(ranks, 1, GROUPS * piece) * (jnp.arange(2) == c).astype(f32)[None, :, None]
    vec_grads = [gb_query, gb_value, sums_one[0], sums_one[1], sums_one[2], sums_two[0], sums_two[1], sums_two[2]]
    vec_parts = jnp.concatenate([v.reshape(ranks, dz) for v in vec_grads] + [gbi.reshape(ranks, fz)], axis=1)
    vec_parts = jnp.pad(vec_parts, ((0, 0), (0, extra * d - nvec))).reshape(ranks, extra, d)

    gw4 = gw_qkv.reshape(ranks, 2, half, 2 * wide)
    keep = lax.dynamic_index_in_dim(gw4, c, 1, keepdims=False)
    give = lax.dynamic_index_in_dim(gw4, 1 - c, 1, keepdims=False)
    gqkv = over_r(keep.astype(f32) + swap(give, "ctx", 1).astype(f32))
    fqkv = scatter_z(jnp.concatenate([gqkv, vec_parts], axis=1))

    def everywhere(x):
        pieces = jnp.stack(over_group(x))
        return jnp.stack([pieces, swap(pieces, "ctx", 1)])

    all_wi, all_wo, all_wout, all_qkv = everywhere(fwi), everywhere(fwo), everywhere(fwout), everywhere(fqkv)
    core_order = c ^ jnp.arange(2)

    def ordered(x):
        return jnp.take(jnp.take(x, core_order, axis=0), group_order, axis=1)

    d_inner = ordered(all_wi).reshape(2 * GROUPS, dz, ranks, piece).transpose(1, 2, 0, 3).reshape(dz, ff)
    d_outer = ordered(all_wo).reshape(fz, d)
    d_out = jnp.take(jnp.sum(all_wout.astype(f32), axis=1), core_order, axis=0)
    d_out = d_out.transpose(1, 0, 2).reshape(dz, d)
    qkv = ordered(all_qkv[:, :, :half])
    qkv = qkv.transpose(0, 2, 1, 3).reshape(dz, GROUPS, 2, per_group, 2, hd).astype(f32)
    d_query = qkv[:, :, 0, :, 0].reshape(dz, d) * 0.125
    d_key = qkv[:, :, 1, :, 0].reshape(dz, d)
    d_value = qkv[:, :, 1, :, 1].reshape(dz, d)
    v_here = jnp.sum(all_qkv[:, :, half:].astype(f32), axis=(0, 1))
    v, d_out_here = v_here, d_out
    for t in range(1, sets // 2):
        v = v + swap(v_here, "ctx", t * 2 * GROUPS)
        d_out = d_out + swap(d_out_here, "ctx", t * 2 * GROUPS)
    v = v.reshape(-1)
    vs = [v[k * dz : (k + 1) * dz] for k in range(8)]

    return (
        result[None],
        grad_input[None],
        d_query,
        vs[0],
        d_key,
        d_value.astype(f32),
        vs[1],
        d_out,
        vs[2],
        vs[3],
        vs[4],
        d_inner.astype(f32),
        v[8 * dz : 8 * dz + fz],
        d_outer.astype(f32),
        vs[5],
        vs[6],
        vs[7],
    )


def solution(mesh):
    rows = P("fsdp", "ctx", None)
    matrix = P("fsdp", None)
    vector = P("fsdp")
    return jax.shard_map(
        per_device,
        mesh=mesh,
        in_specs=(rows, matrix, matrix, vector, matrix, matrix, vector, matrix, vector, vector, vector)
        + (matrix, vector, matrix, vector, vector, vector, rows),
        out_specs=(rows, rows, matrix, vector, matrix, matrix, vector, matrix, vector, vector, vector)
        + (matrix, vector, matrix, vector, vector, vector),
        check_vma=False,
    )
```

time: 1040 us -> 459 us (0.44)
  waiting for transfers between devices: 588 us -> 114 us
  Pallas kernels: 0 us -> 153 us
  matrix products: 142 us -> 0 us
  other arithmetic: 101 us -> 44.8 us
  blocking collectives: 54.4 us -> 0 us
  starting transfers between devices: 32.3 us -> 73 us
  local copies, waits for them, and re-layouts: 97.8 us -> 70.8 us
  between operations: 16.7 us -> 2.13 us
    reduce_scatter x3 -> x0, waiting for transfers between devices: 204 us -> none  [the longest x1 88.3 us: per_device(): lax.psum_scatter(grad_w_inner.astype(jnp.bfloat16), 'fsdp', scatter_dimen...]
    all_gather x8 -> x0, waiting for transfers between devices: 195 us -> none  [the longest x1 78.1 us: per_device(): lax.all_gather(w_outer, 'fsdp', axis=0, tiled=True)]
    pallas_call x0 -> x10, Pallas kernels: none -> 153 us  [the longest x1 50.3 us: per_device(): pl.pallas_call(attend_back_kernel, grid=(GROUPS,), in_specs=[smem, smem,...]
    dot_general x74 -> x0, matrix products: 142 us -> none  [the longest x8 25 us: value_action(): jnp.einsum('shtr,srhd->sthd', weights, value_heads, preferred_element_typ...]
    unnamed x18 -> x0, waiting for transfers between devices: 74.9 us -> none
    convert_element_type x54 -> x14, other arithmetic: 53.5 us -> 8.64 us  [the longest x1 3.82 us: per_device(): d_outer.astype(f32)]
    ppermute x32 -> x74, waiting for transfers between devices: 71.3 us -> 114 us  [swap(): lax.ppermute(x, axis, [(i, i ^ flip) for i in range(lax.axis_size(axis))])]
    psum x1 -> x0, waiting for transfers between devices: 42.1 us -> none  [per_device(): lax.psum(shortened(tuple(shards)), 'ctx')]
  transfers between devices with their start and end apart: 47 -> 74, of which waited for: 38 -> 27; matrix products, arithmetic and copies ran while one was open for 23% -> 16% of each run, Pallas kernels for 0% -> 25%
where the time goes in v1:
time: 459 us; the launch traced here: 458 us
  Pallas kernels  153 us (33%)
  waiting for transfers between devices  114 us (25%)
  starting transfers between devices  73 us (16%)
  local copies, waits for them, and re-layouts  70.8 us (15%)
  other arithmetic  44.8 us (10%)
    ppermute x74, waiting for transfers between devices, swap(): lax.ppermute(x, axis, [(i, i ^ flip) for i in range(lax.axis_size(axis))])  114 us
    ppermute x74, starting transfers between devices, swap(): lax.ppermute(x, axis, [(i, i ^ flip) for i in range(lax.axis_size(axis))])  73 us
    pallas_call x1, Pallas kernels, per_device(): pl.pallas_call(attend_back_kernel, grid=(GROUPS,), in_specs=[smem, smem,...  50.3 us
    pallas_call x1, Pallas kernels, per_device(): pl.pallas_call(attend_kernel, grid=(GROUPS,), in_specs=[smem, smem, stepp...  44 us
    pallas_call x1, Pallas kernels, per_device(): whole_call(feed_weights_kernel, [shape((d, cols), b16)] * GROUPS + [shape...  18.6 us
    unnamed x163, local copies, waits for them, and re-layouts  13.1 us
    gather x8, local copies, waits for them, and re-layouts, ordered(): return jnp.take(jnp.take(x, core_order, axis=0), group_order, axis=1)  10.9 us
  transfers between devices with their start and end apart: 74, of which 27 were waited for; matrix products, arithmetic and copies ran while one was open for 16% of the time, Pallas kernels for 25%

profile of v1, /device:TPU:14, one launch (start us, length us, event | category | flops | bytes accessed | tf_op | source)
XLA Modules:
  0.0 457.8 jit_solution(2666968964954146787)
XLA Ops:
  5.2 2.6 collective-permute-start.4
  11.2 2.7 reshape.266
  26.1 3.5 collective-permute-start.12
  34.0 4.8 %project.1 = (bf16[4,256,384]{2,1,0:T(8,128)(2,1)}, bf16[4,256,384]{2,1,0:T(8,128)(2,1)}, bf16[768,768]{1,0:T(8,128)(2,1)}) custom-call(s32[4]{0:T(128)} %pad_add_fusion.1.sc, bf16[256,768]{1,0:T(8,128)(2,1)} %bitcast.218, bf16[256,768]{1,0:T(8,128)(2,1)} %copy-done.16, bf16[256,768]{1,0:T(8,128)(2,1)} %collective-permute-done.1.t2, ...), custom_call_target="tpu_custom_call" | custom-call | tf_op jit(solution)/shard_map/project/pallas_call | solution.py:433
  41.8 7.6 %collective-permute-done.13 = bf16[192,384]{1,0:T(8,128)(2,1)} collective-permute-done((bf16[192,384]{1,0:T(8,128)(2,1)}, bf16[192,384]{1,0:T(8,128)(2,1)}, u32[]{:S(2)}, u32[]{:S(2)}) %collective-permute-start.13) | collective-permute-done | bytes 147488 | tf_op jit(solution)/shard_map/ppermute | solution.py:20
  52.0 6.9 %collective-permute-done.17 = bf16[192,384]{1,0:T(8,128)(2,1)S(1)} collective-permute-done((bf16[192,384]{1,0:T(8,128)(2,1)}, bf16[192,384]{1,0:T(8,128)(2,1)S(1)}, u32[]{:S(2)}, u32[]{:S(2)}) %collective-permute-start.17) | collective-permute-done | bytes 147488 | tf_op jit(solution)/shard_map/ppermute | solution.py:20
  65.2 2.8 collective-permute-done.24
  71.2 44.0 %attend.1 = (f32[4,256,192]{2,1,0:T(8,128)}, bf16[4,256,192]{2,1,0:T(8,128)(2,1)}, f32[4,8,256]{2,1,0:T(8,128)}) custom-call(s32[4]{0:T(128)} %pad_add_fusion.1.sc, s32[8,2]{1,0:T(8,128)} %copy.99.span, bf16[4,256,384]{2,1,0:T(8,128)(2,1)} %get-tuple-element.63.q, s32[8,1,256]{2,1,0:T(1,128)} %bitcast.260, s32[8,256,128]{2,1,0:T(8,128)} %broadcast_in_dim.99.seg_cols, ...), custom_call_target="tpu_custom_call" | custom-call | tf_op jit(solution)/shard_map/attend/pallas_call | solution.py:462
  130.4 12.6 %collective-permute-done.9.a2 = bf16[256,192]{1,0:T(8,128)(2,1)S(1)} collective-permute-done((bf16[256,192]{1,0:T(8,128)(2,1)S(1)}, bf16[256,192]{1,0:T(8,128)(2,1)S(1)}, u32[]{:S(2)}, u32[]{:S(2)}) %collective-permute-start.9) | collective-permute-done | bytes 98336 | tf_op jit(solution)/shard_map/ppermute | solution.py:20
  143.6 3.8 out.1
  150.6 8.4 %feed.1 = (bf16[4,512,384]{2,1,0:T(8,128)(2,1)}, bf16[4,512,384]{2,1,0:T(8,128)(2,1)}, f32[256,768]{1,0:T(8,128)}, f32[256,768]{1,0:T(8,128)}) custom-call(s32[4]{0:T(128)} %pad_add_fusion.1.sc, bf16[256,768]{1,0:T(8,128)(2,1)} %get-tuple-element.67.n_own, bf16[256,768]{1,0:T(8,128)(2,1)} %copy-done.18, bf16[4,192,384]{2,1,0:T(8,128)(2,1)} %copy-done.4, ...), custom_call_target="tpu_custom_call" | custom-call | tf_op jit(solution)/shard_map/feed/pallas_call | solution.py:489
  163.5 3.6 close.1
  169.8 8.1 %feed_back.1 = (bf16[4,512,384]{2,1,0:T(8,128)(2,1)}, f32[256,768]{1,0:T(8,128)}, f32[256,768]{1,0:T(8,128)}, f32[4,384]{1,0:T(4,128)}) custom-call(s32[4]{0:T(128)} %pad_add_fusion.1.sc, bf16[256,768]{1,0:T(8,128)(2,1)} %get-tuple-element.72.g_own, bf16[256,768]{1,0:T(8,128)(2,1)} %copy-done.15, bf16[4,192,384]{2,1,0:T(8,128)(2,1)} %copy-done.4, ...), custom_call_target="tpu_custom_call" | custom-call | tf_op jit(solution)/shard_map/feed_back/pallas_call | solution.py:511
  177.9 18.6 %feed_weights.1 = (bf16[768,384]{1,0:T(8,128)(2,1)}, bf16[768,384]{1,0:T(8,128)(2,1)}, bf16[768,384]{1,0:T(8,128)(2,1)}, bf16[768,384]{1,0:T(8,128)(2,1)}, bf16[...) custom-call(s32[4]{0:T(128)} %pad_add_fusion.1.sc, ...), custom_call_target="tpu_custom_call" | custom-call | tf_op jit(solution)/shard_map/feed_weights/pallas_call | solution.py:525
  205.0 7.9 %collective-permute-done.55 = bf16[768,384]{1,0:T(8,128)(2,1)S(1)} collective-permute-done((bf16[768,384]{1,0:T(8,128)(2,1)}, bf16[768,384]{1,0:T(8,128)(2,1)S(1)}, u32[]{:S(2)}, u32[]{:S(2)}) %collective-permute-start.55) | collective-permute-done | bytes 589856 | tf_op jit(solution)/shard_map/ppermute | solution.py:20
  216.5 5.5 %first_back.1 = (f32[256,768]{1,0:T(8,128)}, bf16[256,192]{1,0:T(8,128)(2,1)}, bf16[256,192]{1,0:T(8,128)(2,1)}, bf16[256,192]{1,0:T(8,128)(2,1)}, bf16[256,192]...) custom-call(s32[4]{0:T(128)} %pad_add_fusion.1.sc, ...), custom_call_target="tpu_custom_call" | custom-call | tf_op jit(solution)/shard_map/first_back/pallas_call | solution.py:533
  223.4 4.2 collective-permute-done.31
  228.2 18.8 %collective-permute-done.32 = bf16[256,192]{1,0:T(8,128)(2,1)S(1)} collective-permute-done((bf16[256,192]{1,0:T(8,128)(2,1)}, bf16[256,192]{1,0:T(8,128)(2,1)S(1)}, u32[]{:S(2)}, u32[]{:S(2)}) %collective-permute-start.32) | collective-permute-done | bytes 98336 | tf_op jit(solution)/shard_map/ppermute | solution.py:20
  254.1 50.3 %attend_back.1 = (bf16[4,256,384]{2,1,0:T(8,128)(2,1)}, f32[4,256,384]{2,1,0:T(8,128)}, bf16[4,256,384]{2,1,0:T(8,128)(2,1)}) custom-call(s32[4]{0:T(128)} %pad_add_fusion.1.sc, s32[8,2]{1,0:T(8,128)} %copy.99.span, bf16[4,256,384]{2,1,0:T(8,128)(2,1)} %get-tuple-element.63.q, s32[8,1,256]{2,1,0:T(1,128)} %bitcast.261, ...), custom_call_target="tpu_custom_call" | custom-call | tf_op jit(solution)/shard_map/attend_back/pallas_call | solution.py:545
  312.5 4.7 %collective-permute-done.58 = bf16[192,384]{1,0:T(8,128)(2,1)S(1)} collective-permute-done((bf16[192,384]{1,0:T(8,128)(2,1)S(1)}, bf16[192,384]{1,0:T(8,128)(2,1)S(1)}, u32[]{:S(2)}, u32[]{:S(2)}) %collective-permute-start.58) | collective-permute-done | bytes 147488 | tf_op jit(solution)/shard_map/ppermute | solution.py:20
  317.2 3.0 collective-permute-start.69
  320.2 9.9 %collective-permute-done.59 = bf16[192,384]{1,0:T(8,128)(2,1)S(1)} collective-permute-done((bf16[192,384]{1,0:T(8,128)(2,1)S(1)}, bf16[192,384]{1,0:T(8,128)(2,1)S(1)}, u32[]{:S(2)}, u32[]{:S(2)}) %collective-permute-start.59) | collective-permute-done | bytes 147488 | tf_op jit(solution)/shard_map/ppermute | solution.py:20
  343.2 4.5 collective-permute-done.48
  357.6 6.4 %project_back.1 = (f32[256,768]{1,0:T(8,128)}, bf16[3,256,768]{2,1,0:T(8,128)(2,1)}, bf16[768,768]{1,0:T(8,128)(2,1)}, f32[1,768]{1,0:T(1,128)}) custom-call(s32[4]{0:T(128)} %pad_add_fusion.1.sc, bf16[256,768]{1,0:T(8,128)(2,1)} %bitcast.220, bf16[256,768]{1,0:T(8,128)(2,1)} %copy-done.16, bf16[256,768]{1,0:T(8,128)(2,1)} %collective-permute-done.1.t2, ...), custom_call_target="tpu_custom_call" | custom-call | tf_op jit(solution)/shard_map/project_back/pallas_call | solution.py:566
  370.3 3.5 collective-permute-start.39
  380.7 5.1 %collective-permute-done.40 = bf16[104,768]{1,0:T(8,128)(2,1)} collective-permute-done((bf16[104,768]{1,0:T(8,128)(2,1)}, bf16[104,768]{1,0:T(8,128)(2,1)}, u32[]{:S(2)}, u32[]{:S(2)}) %collective-permute-start.40) | collective-permute-done | bytes 159776 | tf_op jit(solution)/shard_map/ppermute | solution.py:20
  385.8 4.5 collective-permute-done.41
  413.1 3.1 reshape.282
  437.7 3.8 bitcast_convert_fusion
  441.5 4.0 copy.103
  445.5 3.2 reshape.281
  448.7 2.8 fusion.33
  (443 shorter events, 180.8 us)
Async XLA Ops:
  8.3 21.3 %collective-permute-start = (bf16[256,768]{1,0:T(8,128)(2,1)S(1)}, bf16[256,768]{1,0:T(8,128)(2,1)S(1)}, u32[]{:S(2)}, u32[]{:S(2)}) collective-permute-start(bf16[256,768]{1,0:T(8,128)(2,1)S(1)} %bitcast.221), channel_id=1, source_target_pairs={{0,8},{4,12},{8,0},{12,4},{16,24},{20,28},{24,16},{28,20},{1,9},{5... | collective-permute-start | bytes 1179656 | tf_op jit(solution)/shard_map/ppermute | solution.py:20
  8.8 20.7 %collective-permute-start.1 = (bf16[256,768]{1,0:T(8,128)(2,1)S(1)}, bf16[256,768]{1,0:T(8,128)(2,1)}, u32[]{:S(2)}, u32[]{:S(2)}) collective-permute-start(bf16[256,768]{1,0:T(8,128)(2,1)S(1)} %bitcast.222), channel_id=1, source_target_pairs={{0,16},{4,20},{8,24},{12,28},{16,0},{20,4},{24,8},{28,12},{1,17},{... | collective-permute-start | bytes 1179656 | tf_op jit(solution)/shard_map/ppermute | solution.py:20
  29.6 19.9 %collective-permute-start.13 = (bf16[192,384]{1,0:T(8,128)(2,1)}, bf16[192,384]{1,0:T(8,128)(2,1)}, u32[]{:S(2)}, u32[]{:S(2)}) collective-permute-start(bf16[192,384]{1,0:T(8,128)(2,1)} %constant_dynamic-slice_fusion.2), channel_id=1, source_target_pairs={{0,3},{1,2},{2,1},{3,0},{4,7},{5,6},{6,5},{7,4},{8,11},{9,10},{10,... | collective-permute-start | bytes 442376 | tf_op jit(solution)/shard_map/ppermute | solution.py:20
  29.6 19.9 %collective-permute-start.16 = (bf16[192,384]{1,0:T(8,128)(2,1)}, bf16[192,384]{1,0:T(8,128)(2,1)S(1)}, u32[]{:S(2)}, u32[]{:S(2)}) collective-permute-start(bf16[192,384]{1,0:T(8,128)(2,1)} %reshape.267), channel_id=1, source_target_pairs={{0,1},{1,0},{2,3},{3,2},{4,5},{5,4},{6,7},{7,6},{8,9},{9,8},{10,11... | collective-permute-start | bytes 442376 | tf_op jit(solution)/shard_map/ppermute | solution.py:20
  31.1 27.8 %collective-permute-start.17 = (bf16[192,384]{1,0:T(8,128)(2,1)}, bf16[192,384]{1,0:T(8,128)(2,1)S(1)}, u32[]{:S(2)}, u32[]{:S(2)}) collective-permute-start(bf16[192,384]{1,0:T(8,128)(2,1)} %reshape.267), channel_id=1, source_target_pairs={{0,2},{1,3},{2,0},{3,1},{4,6},{5,7},{6,4},{7,5},{8,10},{9,11},{10,... | collective-permute-start | bytes 442376 | tf_op jit(solution)/shard_map/ppermute | solution.py:20
  33.2 28.9 %collective-permute-start.18 = (bf16[192,384]{1,0:T(8,128)(2,1)}, bf16[192,384]{1,0:T(8,128)(2,1)}, u32[]{:S(2)}, u32[]{:S(2)}) collective-permute-start(bf16[192,384]{1,0:T(8,128)(2,1)} %reshape.267), channel_id=1, source_target_pairs={{0,3},{1,2},{2,1},{3,0},{4,7},{5,6},{6,5},{7,4},{8,11},{9,10},{10,... | collective-permute-start | bytes 442376 | tf_op jit(solution)/shard_map/ppermute | solution.py:20
  40.2 22.9 %collective-permute-start.22 = (bf16[96,768]{1,0:T(8,128)(2,1)}, bf16[96,768]{1,0:T(8,128)(2,1)S(1)}, u32[]{:S(2)}, u32[]{:S(2)}) collective-permute-start(bf16[96,768]{1,0:T(8,128)(2,1)} %constant_dynamic-slice_fusion), channel_id=1, source_target_pairs={{0,1},{1,0},{2,3},{3,2},{4,5},{5,4},{6,7},{7,6},{8,9},{9,8},{10,11... | collective-permute-start | bytes 442376 | tf_op jit(solution)/shard_map/ppermute | solution.py:20
  49.5 18.5 %collective-permute-start.24 = (bf16[96,768]{1,0:T(8,128)(2,1)}, bf16[96,768]{1,0:T(8,128)(2,1)S(1)}, u32[]{:S(2)}, u32[]{:S(2)}) collective-permute-start(bf16[96,768]{1,0:T(8,128)(2,1)} %constant_dynamic-slice_fusion), channel_id=1, source_target_pairs={{0,3},{1,2},{2,1},{3,0},{4,7},{5,6},{6,5},{7,4},{8,11},{9,10},{10,... | collective-permute-start | bytes 442376 | tf_op jit(solution)/shard_map/ppermute | solution.py:20
  62.1 57.9 %collective-permute-start.14 = (bf16[4,192,384]{2,1,0:T(8,128)(2,1)S(1)}, bf16[4,192,384]{2,1,0:T(8,128)(2,1)}, u32[]{:S(2)}, u32[]{:S(2)}) collective-permute-start(bf16[4,192,384]{2,1,0:T(8,128)(2,1)S(1)} %pad_maximum_fusion.5.own), channel_id=1, source_target_pairs={{0,4},{4,0},{8,12},{12,8},{16,20},{20,16},{24,28},{28,24},{1,5},{5... | collective-permute-start | bytes 1769480 | tf_op jit(solution)/shard_map/ppermute | solution.py:20
  63.1 57.4 %collective-permute-start.19 = (bf16[4,192,384]{2,1,0:T(8,128)(2,1)S(1)}, bf16[4,192,384]{2,1,0:T(8,128)(2,1)S(1)}, u32[]{:S(2)}, u32[]{:S(2)}) collective-permute-start(bf16[4,192,384]{2,1,0:T(8,128)(2,1)S(1)} %pad_maximum_fusion.6.i0), channel_id=1, source_target_pairs={{0,8},{4,12},{8,0},{12,4},{16,24},{20,28},{24,16},{28,20},{1,9},{5... | collective-permute-start | bytes 1769480 | tf_op jit(solution)/shard_map/ppermute | solution.py:20
  68.1 53.0 %collective-permute-start.26 = (bf16[4,96,768]{2,1,0:T(8,128)(2,1)S(1)}, bf16[4,96,768]{2,1,0:T(8,128)(2,1)}, u32[]{:S(2)}, u32[]{:S(2)}) collective-permute-start(bf16[4,96,768]{2,1,0:T(8,128)(2,1)S(1)} %pad_maximum_fusion.7.o0), channel_id=1, source_target_pairs={{0,16},{4,20},{8,24},{12,28},{16,0},{20,4},{24,8},{28,12},{1,17},{... | collective-permute-start | bytes 1769480 | tf_op jit(solution)/shard_map/ppermute | solution.py:20
  120.0 28.9 %collective-permute-start.20 = (bf16[4,192,384]{2,1,0:T(8,128)(2,1)S(1)}, bf16[4,192,384]{2,1,0:T(8,128)(2,1)S(1)}, u32[]{:S(2)}, u32[]{:S(2)}) collective-permute-start(bf16[4,192,384]{2,1,0:T(8,128)(2,1)S(1)} %pad_maximum_fusion.6.i0), channel_id=1, source_target_pairs={{0,16},{4,20},{8,24},{12,28},{16,0},{20,4},{24,8},{28,12},{1,17},{... | collective-permute-start | bytes 1769480 | tf_op jit(solution)/shard_map/ppermute | solution.py:20
  120.5 28.3 %collective-permute-start.25 = (bf16[4,96,768]{2,1,0:T(8,128)(2,1)S(1)}, bf16[4,96,768]{2,1,0:T(8,128)(2,1)S(1)}, u32[]{:S(2)}, u32[]{:S(2)}) collective-permute-start(bf16[4,96,768]{2,1,0:T(8,128)(2,1)S(1)} %pad_maximum_fusion.7.o0), channel_id=1, source_target_pairs={{0,8},{4,12},{8,0},{12,4},{16,24},{20,28},{24,16},{28,20},{1,9},{5... | collective-permute-start | bytes 1769480 | tf_op jit(solution)/shard_map/ppermute | solution.py:20
  121.1 27.8 %collective-permute-start.21 = (bf16[4,192,384]{2,1,0:T(8,128)(2,1)S(1)}, bf16[4,192,384]{2,1,0:T(8,128)(2,1)}, u32[]{:S(2)}, u32[]{:S(2)}) collective-permute-start(bf16[4,192,384]{2,1,0:T(8,128)(2,1)S(1)} %collective-permute-done.19.i1), channel_id=1, source_target_pairs={{0,16},{4,20},{8,24},{12,28},{16,0},{20,4},{24,8},{28,12},{1,17},{... | collective-permute-start | bytes 1769480 | tf_op jit(solution)/shard_map/ppermute | solution.py:20
  124.4 24.5 %collective-permute-start.27 = (bf16[4,96,768]{2,1,0:T(8,128)(2,1)}, bf16[4,96,768]{2,1,0:T(8,128)(2,1)}, u32[]{:S(2)}, u32[]{:S(2)}) collective-permute-start(bf16[4,96,768]{2,1,0:T(8,128)(2,1)} %collective-permute-done.26.o2), channel_id=1, source_target_pairs={{0,8},{4,12},{8,0},{12,4},{16,24},{20,28},{24,16},{28,20},{1,9},{5... | collective-permute-start | bytes 1769480 | tf_op jit(solution)/shard_map/ppermute | solution.py:20
  200.6 103.7 %collective-permute-start.54 = (bf16[768,384]{1,0:T(8,128)(2,1)}, bf16[768,384]{1,0:T(8,128)(2,1)}, u32[]{:S(2)}, u32[]{:S(2)}) collective-permute-start(bf16[768,384]{1,0:T(8,128)(2,1)} %get-tuple-element.100), channel_id=1, source_target_pairs={{0,8},{4,12},{8,0},{12,4},{16,24},{20,28},{24,16},{28,20},{1,9},{5... | collective-permute-start | bytes 1769480 | tf_op jit(solution)/shard_map/ppermute | solution.py:20
  202.9 19.7 %collective-permute-start.64 = (bf16[384,768]{1,0:T(8,128)(2,1)}, bf16[384,768]{1,0:T(8,128)(2,1)S(1)}, u32[]{:S(2)}, u32[]{:S(2)}) collective-permute-start(bf16[384,768]{1,0:T(8,128)(2,1)} %get-tuple-element.105), channel_id=1, source_target_pairs={{0,16},{4,20},{8,24},{12,28},{16,0},{20,4},{24,8},{28,12},{1,17},{... | collective-permute-start | bytes 1769480 | tf_op jit(solution)/shard_map/ppermute | solution.py:20
  204.3 102.9 %collective-permute-start.66 = (bf16[384,768]{1,0:T(8,128)(2,1)}, bf16[384,768]{1,0:T(8,128)(2,1)S(1)}, u32[]{:S(2)}, u32[]{:S(2)}) collective-permute-start(bf16[384,768]{1,0:T(8,128)(2,1)} %get-tuple-element.106), channel_id=1, source_target_pairs={{0,16},{4,20},{8,24},{12,28},{16,0},{20,4},{24,8},{28,12},{1,17},{... | collective-permute-start | bytes 1769480 | tf_op jit(solution)/shard_map/ppermute | solution.py:20
  214.1 90.2 %collective-permute-start.56 = (bf16[768,384]{1,0:T(8,128)(2,1)S(1)}, bf16[768,384]{1,0:T(8,128)(2,1)}, u32[]{:S(2)}, u32[]{:S(2)}) collective-permute-start(bf16[768,384]{1,0:T(8,128)(2,1)S(1)} %add_convert_fusion.1), channel_id=1, source_target_pairs={{0,16},{4,20},{8,24},{12,28},{16,0},{20,4},{24,8},{28,12},{1,17},{... | collective-permute-start | bytes 1769480 | tf_op jit(solution)/shard_map/ppermute | solution.py:20
  222.6 24.3 %collective-permute-start.32 = (bf16[256,192]{1,0:T(8,128)(2,1)}, bf16[256,192]{1,0:T(8,128)(2,1)S(1)}, u32[]{:S(2)}, u32[]{:S(2)}) collective-permute-start(bf16[256,192]{1,0:T(8,128)(2,1)} %get-tuple-element.80), channel_id=1, source_target_pairs={{0,16},{4,20},{8,24},{12,28},{16,0},{20,4},{24,8},{28,12},{1,17},{... | collective-permute-start | bytes 294920 | tf_op jit(solution)/shard_map/ppermute | solution.py:20
  227.6 82.0 %collective-permute-start.65 = (bf16[384,768]{1,0:T(8,128)(2,1)S(1)}, bf16[384,768]{1,0:T(8,128)(2,1)}, u32[]{:S(2)}, u32[]{:S(2)}) collective-permute-start(bf16[384,768]{1,0:T(8,128)(2,1)S(1)} %add_convert_fusion), channel_id=1, source_target_pairs={{0,8},{4,12},{8,0},{12,4},{16,24},{20,28},{24,16},{28,20},{1,9},{5... | collective-permute-start | bytes 1769480 | tf_op jit(solution)/shard_map/ppermute | solution.py:20
  253.2 77.7 %collective-permute-start.46 = (bf16[768,384]{1,0:T(8,128)(2,1)}, bf16[768,384]{1,0:T(8,128)(2,1)S(1)}, u32[]{:S(2)}, u32[]{:S(2)}) collective-permute-start(bf16[768,384]{1,0:T(8,128)(2,1)} %get-tuple-element.96), channel_id=1, source_target_pairs={{0,4},{4,0},{8,12},{12,8},{16,20},{20,16},{24,28},{28,24},{1,5},{5... | collective-permute-start | bytes 1769480 | tf_op jit(solution)/shard_map/ppermute | solution.py:20
  307.2 23.0 %collective-permute-start.59 = (bf16[192,384]{1,0:T(8,128)(2,1)S(1)}, bf16[192,384]{1,0:T(8,128)(2,1)S(1)}, u32[]{:S(2)}, u32[]{:S(2)}) collective-permute-start(bf16[192,384]{1,0:T(8,128)(2,1)S(1)} %get-tuple-element.204), channel_id=1, source_target_pairs={{0,3},{1,2},{2,1},{3,0},{4,7},{5,6},{6,5},{7,4},{8,11},{9,10},{10,... | collective-permute-start | bytes 442376 | tf_op jit(solution)/shard_map/ppermute | solution.py:20
  310.9 21.5 %collective-permute-start.67 = (bf16[96,768]{1,0:T(8,128)(2,1)S(1)}, bf16[96,768]{1,0:T(8,128)(2,1)S(1)}, u32[]{:S(2)}, u32[]{:S(2)}) collective-permute-start(bf16[96,768]{1,0:T(8,128)(2,1)S(1)} %get-tuple-element.198), channel_id=1, source_target_pairs={{0,1},{1,0},{2,3},{3,2},{4,5},{5,4},{6,7},{7,6},{8,9},{9,8},{10,11... | collective-permute-start | bytes 442376 | tf_op jit(solution)/shard_map/ppermute | solution.py:20
  312.0 21.6 %collective-permute-start.68 = (bf16[96,768]{1,0:T(8,128)(2,1)S(1)}, bf16[96,768]{1,0:T(8,128)(2,1)S(1)}, u32[]{:S(2)}, u32[]{:S(2)}) collective-permute-start(bf16[96,768]{1,0:T(8,128)(2,1)S(1)} %get-tuple-element.200), channel_id=1, source_target_pairs={{0,2},{1,3},{2,0},{3,1},{4,6},{5,7},{6,4},{7,5},{8,10},{9,11},{10,... | collective-permute-start | bytes 442376 | tf_op jit(solution)/shard_map/ppermute | solution.py:20
  317.2 17.9 %collective-permute-start.69 = (bf16[96,768]{1,0:T(8,128)(2,1)S(1)}, bf16[96,768]{1,0:T(8,128)(2,1)S(1)}, u32[]{:S(2)}, u32[]{:S(2)}) collective-permute-start(bf16[96,768]{1,0:T(8,128)(2,1)S(1)} %get-tuple-element.199), channel_id=1, source_target_pairs={{0,3},{1,2},{2,1},{3,0},{4,7},{5,6},{6,5},{7,4},{8,11},{9,10},{10,... | collective-permute-start | bytes 442376 | tf_op jit(solution)/shard_map/ppermute | solution.py:20
  333.5 23.2 %collective-permute-start.34 = (bf16[4,256,384]{2,1,0:T(8,128)(2,1)S(1)}, bf16[4,256,384]{2,1,0:T(8,128)(2,1)S(1)}, u32[]{:S(2)}, u32[]{:S(2)}) collective-permute-start(bf16[4,256,384]{2,1,0:T(8,128)(2,1)S(1)} %copy-done.72), channel_id=1, source_target_pairs={{0,4},{4,0},{8,12},{12,8},{16,20},{20,16},{24,28},{28,24},{1,5},{5... | collective-permute-start | bytes 2359304 | tf_op jit(solution)/shard_map/ppermute | solution.py:20
  351.8 24.5 %collective-permute-start.63 = (bf16[4,192,384]{2,1,0:T(8,128)(2,1)S(1)}, bf16[4,192,384]{2,1,0:T(8,128)(2,1)}, u32[]{:S(2)}, u32[]{:S(2)}) collective-permute-start(bf16[4,192,384]{2,1,0:T(8,128)(2,1)S(1)} %get-tuple-element.202), channel_id=1, source_target_pairs={{0,4},{4,0},{8,12},{12,8},{16,20},{20,16},{24,28},{28,24},{1,5},{5... | collective-permute-start | bytes 1769480 | tf_op jit(solution)/shard_map/ppermute | solution.py:20
  356.7 52.4 %collective-permute-start.73 = (bf16[4,96,768]{2,1,0:T(8,128)(2,1)}, bf16[4,96,768]{2,1,0:T(8,128)(2,1)}, u32[]{:S(2)}, u32[]{:S(2)}) collective-permute-start(bf16[4,96,768]{2,1,0:T(8,128)(2,1)} %get-tuple-element.197), channel_id=1, source_target_pairs={{0,4},{4,0},{8,12},{12,8},{16,20},{20,16},{24,28},{28,24},{1,5},{5... | collective-permute-start | bytes 1769480 | tf_op jit(solution)/shard_map/ppermute | solution.py:20
  376.3 46.8 %collective-permute-start.53 = (bf16[4,192,384]{2,1,0:T(8,128)(2,1)}, bf16[4,192,384]{2,1,0:T(8,128)(2,1)}, u32[]{:S(2)}, u32[]{:S(2)}) collective-permute-start(bf16[4,192,384]{2,1,0:T(8,128)(2,1)} %get-tuple-element.207), channel_id=1, source_target_pairs={{0,4},{4,0},{8,12},{12,8},{16,20},{20,16},{24,28},{28,24},{1,5},{5... | collective-permute-start | bytes 1769480 | tf_op jit(solution)/shard_map/ppermute | solution.py:20
  399.3 19.0 %collective-permute-start.35 = (bf16[256,768]{1,0:T(8,128)(2,1)}, bf16[256,768]{1,0:T(8,128)(2,1)}, u32[]{:S(2)}, u32[]{:S(2)}) collective-permute-start(bf16[256,768]{1,0:T(8,128)(2,1)} %get-tuple-element.188), channel_id=1, source_target_pairs={{0,8},{4,12},{8,0},{12,4},{16,24},{20,28},{24,16},{28,20},{1,9},{5... | collective-permute-start | bytes 1179656 | tf_op jit(solution)/shard_map/ppermute | solution.py:20
  409.1 17.1 %collective-permute-start.45 = (bf16[4,104,768]{2,1,0:T(8,128)(2,1)}, bf16[4,104,768]{2,1,0:T(8,128)(2,1)}, u32[]{:S(2)}, u32[]{:S(2)}) collective-permute-start(bf16[4,104,768]{2,1,0:T(8,128)(2,1)} %get-tuple-element.191), channel_id=1, source_target_pairs={{0,4},{4,0},{8,12},{12,8},{16,20},{20,16},{24,28},{28,24},{1,5},{5... | collective-permute-start | bytes 1916936 | tf_op jit(solution)/shard_map/ppermute | solution.py:20
  (116 other events, 1200.5 us)

commit v2 on v1

v2 whole, which is shorter than its diff:
```python
import functools
import math

import jax
import jax.numpy as jnp
from jax import lax
from jax.experimental import pallas as pl
from jax.experimental.pallas import tpu as pltpu
from jax.sharding import PartitionSpec as P

HEADS = 12
GROUPS = 4
LN_EPS = 1e-12
MASKED = -1e30
f32 = jnp.float32
b16 = jnp.bfloat16


def swap(x, axis, flip):
    return lax.ppermute(x, axis, [(i, i ^ flip) for i in range(lax.axis_size(axis))])


def after(x, *others):
    return lax.optimization_barrier((x,) + others)[0]


def nn(a, b):
    return lax.dot_general(a, b, (((1,), (0,)), ((), ())), preferred_element_type=f32)


def nt(a, b):
    return lax.dot_general(a, b, (((1,), (1,)), ((), ())), preferred_element_type=f32)


def tn(a, b):
    return lax.dot_general(a, b, (((0,), (0,)), ((), ())), preferred_element_type=f32)


COSTS = dict(
    pack_first=2, pack_feed=3, split_second=1, vectors=2, project=5, attend=11, out=4, feed=8, close=4, feed_back=8, feed_weights_far=4, first_back=4,
    out_weights=3, feed_weights=7, attend_back=22, project_weights=6, spread=3, spread_feed=3, spread_out=2, project_back=4,
    finish=3, finish_feed=5,
)


def cost(name):
    return pl.CostEstimate(flops=COSTS[name] * 10**10, bytes_accessed=10**6, transcendentals=0)


def whole_call(body, outs, n_in, scratch=(), name=None):
    specs = [pl.BlockSpec(memory_space=pltpu.SMEM)]
    specs += [pl.BlockSpec(memory_space=pltpu.VMEM)] * (n_in - 1)
    return pl.pallas_call(
        body,
        out_shape=outs,
        in_specs=specs,
        out_specs=[pl.BlockSpec(memory_space=pltpu.VMEM)] * len(outs),
        scratch_shapes=list(scratch),
        name=name,
        cost_estimate=cost(name),
    )


def shape(dims, dtype):
    return jax.ShapeDtypeStruct(dims, dtype)


def row_sum(x):
    return jnp.sum(x, axis=0, keepdims=True)


def normalised(x):
    center = x - jnp.mean(x, axis=-1, keepdims=True)
    spread = jnp.mean(center * center, axis=-1, keepdims=True)
    rate = lax.rsqrt(spread + LN_EPS)
    return center * rate, rate


def norm_back(u, hat, rate):
    along = jnp.mean(u * hat, axis=-1, keepdims=True)
    return rate * (u - jnp.mean(u, axis=-1, keepdims=True) - hat * along)


def pack_first_kernel(sc, wq, wk, wv, v0, v1, v2, v3, v4, v5, v6, v7, v8, out):
    c, g = sc[1], sc[3]
    half = wq.shape[0] // 2
    d = out.shape[1]
    gw, hd = d // GROUPS, d // HEADS
    at = pl.ds(pl.multiple_of(c * half, 16), half)
    gap = jnp.zeros((half, hd), b16)
    for k in range(GROUPS):

        @pl.when(g == k)
        def _(k=k):
            parts = []
            for h in range(gw // hd):
                lanes = slice(k * gw + h * hd, k * gw + (h + 1) * hd)
                parts += [wq[at, lanes] * jnp.asarray(0.125, b16), gap]
            for h in range(gw // hd):
                lanes = slice(k * gw + h * hd, k * gw + (h + 1) * hd)
                parts += [wk[at, lanes], wv[at, lanes]]
            out[:half] = jnp.concatenate(parts, axis=1)

    dz = v0.shape[0]
    each = d // dz
    cells = [v[...].reshape(1, -1) for v in (v0, v1, v2, v3, v4, v5, v6, v7, v8)]
    cells.append(jnp.zeros((1, d - v8.shape[0] % d), b16))
    lines, line, used = [], [], 0
    for cell in cells:
        line.append(cell)
        used += cell.shape[1]
        if used == d:
            lines.append(jnp.concatenate(line, axis=1))
            line, used = [], 0
    lines.append(jnp.zeros((8 - len(lines), d), b16))
    out[half:] = jnp.concatenate(lines, axis=0)


def pack_feed_kernel(sc, w_in, w_outer, w_out, inner, second):
    c, g = sc[1], sc[3]
    piece = second.shape[0] - w_out.shape[0] // 2
    ranks = inner.shape[1] // piece
    span = 2 * GROUPS * piece
    half, width = w_out.shape[0] // 2, w_out.shape[1] // 2
    own = c * GROUPS + g
    for k in range(2 * GROUPS):

        @pl.when(own == k)
        def _(k=k):
            lanes = [slice(y * span + k * piece, y * span + (k + 1) * piece) for y in range(ranks)]
            inner[...] = jnp.concatenate([w_in[:, at] for at in lanes], axis=1)

    second[:piece] = w_outer[pl.ds(pl.multiple_of(own * piece, 16), piece), :]
    for core in range(2):

        @pl.when(c == core)
        def _(core=core):
            for side in range(2):
                part = w_out[side * half : (side + 1) * half, core * width : (core + 1) * width]
                second[piece:, side * width : (side + 1) * width] = part


def split_second_kernel(sc, *refs):
    outer, out = refs[-2:]
    piece = outer.shape[1]
    for a, part in enumerate(refs[:-2]):
        outer[a] = part[:piece]
        out[a] = part[piece:]


def project_kernel(sc, t0, t1, t2, t3, own, par, shift, q_out, kv_out, w_out):
    z, c = sc[0], sc[1]
    ranks, half = own.shape[0], own.shape[1]
    width = q_out.shape[-1]
    for a in range(ranks):
        base = (z ^ a) * (2 * half)
        w_out[pl.ds(pl.multiple_of(base + c * half, 16), half), :] = own[a]
        w_out[pl.ds(pl.multiple_of(base + (1 - c) * half, 16), half), :] = par[a]
    for s, t in enumerate((t0, t1, t2, t3)):
        y = nn(t[...], w_out[...]) + shift[...]
        q_out[s] = y[:, :width].astype(b16)
        kv_out[s] = y[:, width:].astype(b16)


def project_weights_kernel(sc, t0, t1, t2, t3, dq_far, dq_near, dkv, dkv_in, sums_one, sums_two, keep, give, sums, both, total):
    ranks, half = keep.shape[0], give.shape[1]
    c = sc[1]
    width = dq_far.shape[-1]
    dqs = (dq_near[1], dq_near[0], dq_far[1], dq_far[0])
    column = jnp.zeros((1, 2 * width), f32)
    for s, t in enumerate((t0, t1, t2, t3)):
        both[s, :, :width] = dqs[s]
        both[s, :, width:] = (dkv[s] + dkv_in[s].astype(f32)).astype(b16)
        column += row_sum(both[s].astype(f32))
    total[...] = nn(jnp.concatenate([t0[...], t1[...], t2[...], t3[...]], axis=0).T, both[...].reshape(-1, 2 * width))
    for a in range(ranks):
        base = a * 2 * half
        keep[a] = total[pl.ds(pl.multiple_of(base + c * half, 16), half), :]
        give[a] = total[pl.ds(pl.multiple_of(base + (1 - c) * half, 16), half), :].astype(b16)
    sums[...] = jnp.concatenate([column, sums_one[0:3], sums_two[0:3], jnp.zeros((1, 2 * width), f32)], axis=0)


def project_back_kernel(sc, both, w, grad_one, dx_own, dx1, dx2, dx3):
    dx_own[...] = grad_one[...] + nt(both[0], w[...])
    for s, out in ((1, dx1), (2, dx2), (3, dx3)):
        out[...] = nt(both[s], w[...]).astype(b16)


def spread_kernel(sc, keep, got, sums, own, *sends):
    z = sc[0]
    half = got.shape[1]
    own[:half] = keep[z] + got[z].astype(f32)
    own[half:] = sums[...]
    for a, send in enumerate(sends):
        send[:half] = (keep[z ^ (a + 1)] + got[z ^ (a + 1)].astype(f32)).astype(b16)
        send[half:] = sums[...].astype(b16)


def spread_feed_kernel(sc, mine, left, right, own, *sends):
    z = sc[0]
    for a, out in enumerate((own,) + sends):
        k = z ^ a
        out[...] = (mine[k].astype(f32) + left[k].astype(f32) + right[k].astype(f32)).astype(out.dtype)


def spread_out_kernel(sc, mine, other, own, *sends):
    z = sc[0]
    for a, out in enumerate((own,) + sends):
        out[...] = (mine[z ^ a].astype(f32) + other[z ^ a].astype(f32)).astype(out.dtype)


def vectors_kernel(sc, rows, outs, shift_qkv, shift_inner, full, inner):
    z, c, g = sc[0], sc[1], sc[3]
    ranks = rows.shape[0]
    d = full.shape[1]
    dz = d // ranks
    piece = inner.shape[1] // ranks
    for k in range(ranks):
        row = rows[z ^ k].astype(f32)
        each = d // dz
        for j in range(8):
            low = (j % each) * dz
            full[j : j + 1, k * dz : (k + 1) * dz] = row[j // each : j // each + 1, low : low + dz]
        last = row[8 // each : 8 // each + 1]
        for j in range(2 * GROUPS):
            inner[j : j + 1, k * piece : (k + 1) * piece] = last[:, j * piece : (j + 1) * piece]
    outs[...] = full[...]
    gw = d // GROUPS
    hd = d // HEADS
    query, value = jnp.zeros((1, gw), f32), jnp.zeros((1, gw), f32)
    for k in range(GROUPS):
        query = jnp.where(g == k, full[0:1, k * gw : (k + 1) * gw], query)
        value = jnp.where(g == k, full[1:2, k * gw : (k + 1) * gw], value)
    gap = jnp.zeros((1, hd), f32)
    parts = []
    for h in range(gw // hd):
        parts += [query[:, h * hd : (h + 1) * hd] * 0.125, gap]
    for h in range(gw // hd):
        parts += [gap, value[:, h * hd : (h + 1) * hd]]
    shift_qkv[...] = jnp.concatenate(parts, axis=1)
    for s in range(GROUPS):
        shift_inner[s : s + 1, :] = inner[pl.ds(c * GROUPS + (g ^ s), 1), :]


def block_of(sc, entry, s):
    rank = sc[2] ^ entry
    return ((rank >> 1) * GROUPS + (sc[3] ^ s)) * 2 + (rank & 1)


def gather_blocks(sc, parts, kv_all):
    @pl.when(pl.program_id(0) == 0)
    def _():
        for entry, part in enumerate(parts):
            for s in range(GROUPS):
                kv_all[block_of(sc, entry, s)] = part[s]


def attend_kernel(start, sc, span, q, seg_rows, seg_cols, *rest):
    parts, (mixed, low_out, log_out), (kv_all, kept, top, acc) = rest[:-7], rest[-7:-4], rest[-4:]
    gather_blocks(sc, parts, kv_all)
    here = block_of(sc, 0, start - pl.program_id(0))
    low, high = span[here, 0], span[here, 1]
    rows = q.shape[1]
    per_group = q.shape[2] // 128
    left = lax.broadcasted_iota(jnp.int32, (rows, 128), 1) < 64
    one = jnp.ones((rows, 128), b16)
    seg_q = seg_cols[here]
    for h in range(per_group):
        top[h] = jnp.full((rows, 128), MASKED, f32)
        acc[h] = jnp.zeros((rows, 128), f32)

    @pl.loop(low, high)
    def _(j):
        seg = seg_rows[j]
        for h in range(per_group):
            lanes = slice(h * 128, (h + 1) * 128)
            s = nt(q[0, :, lanes], kv_all[j, :, lanes])
            best = top[h]
            for w in range(0, rows, 128):
                part = jnp.where(seg_q == seg[:, w : w + 128], s[:, w : w + 128], MASKED)
                kept[h, j, :, w : w + 128] = part
                best = jnp.maximum(best, part)
            top[h] = best

    for h in range(per_group):
        top[h] = jnp.broadcast_to(jnp.max(top[h], axis=1, keepdims=True), (rows, 128))

    @pl.loop(low, high)
    def _(j):
        for h in range(per_group):
            lanes = slice(h * 128, (h + 1) * 128)
            m = top[h]
            p = jnp.concatenate([jnp.exp(kept[h, j, :, w : w + 128] - m).astype(b16) for w in range(0, rows, 128)], axis=1)
            acc[h] += nn(p, jnp.where(left, one, kv_all[j, :, lanes]))

    log_out[...] = jnp.zeros(log_out.shape, f32)
    for h in range(per_group):
        a = acc[h]
        out = a[:, 64:] / a[:, :64]
        mixed[0, :, h * 64 : (h + 1) * 64] = out
        low_out[0, :, h * 64 : (h + 1) * 64] = out.astype(b16)
        log = top[h] + jnp.log(jnp.broadcast_to(a[:, 0:1], (rows, 128)))
        log_out[0, h : h + 1, :] = jnp.transpose(log)[0:1]


def attend_back_kernel(start, sc, span, q, seg_rows, seg_cols, *rest):
    count, begins, ends = start[1], start[2], start[3]
    grads, rest = rest[:count], rest[count:]
    mixed, logs = rest[:2]
    spare = len(rest) - (7 if begins else 8)
    sets = spare // 2 if ends else spare - 1
    parts, rest = rest[2 : 2 + sets], rest[2 + sets :]
    if not begins:
        before, rest = rest[0], rest[1:]
    dq, dkv_out, dkv_send = rest[0], rest[1], rest[2:-4]
    kv_all, dkv_all, dq_acc, both = rest[-4:]
    step = pl.program_id(0)
    gather_blocks(sc, parts, kv_all)

    @pl.when(step == 0)
    def _():
        dkv_all[...] = jnp.zeros(dkv_all.shape, f32) if begins else before[...]

    here = block_of(sc, 0, start[0] - step)
    low, high = span[here, 0], span[here, 1]
    rows = q.shape[1]
    per_group = q.shape[2] // 128
    seg_q = seg_rows[here]
    gap = jnp.zeros((rows, 64), b16)
    grad = grads[0][...]
    for k in range(1, count):
        grad = jnp.where(step == k, grads[k][...], grad)
    balance = []
    for h in range(per_group):
        part = slice(h * 64, (h + 1) * 64)
        gh = grad[:, part]
        along = jnp.sum(gh.astype(f32) * mixed[0, :, part], axis=1, keepdims=True)
        balance.append(jnp.transpose(jnp.broadcast_to(along, (rows, 128)))[0:1])
        both[h, :rows] = q[0, :, h * 128 : (h + 1) * 128]
        both[h, rows:] = jnp.concatenate([gap, gh], axis=1)
        dq_acc[h] = jnp.zeros((rows, 128), f32)

    @pl.loop(low, high)
    def _(j):
        seg = seg_cols[j]
        ok = jnp.concatenate([seg == seg_q[:, w : w + 128] for w in range(0, rows, 128)], axis=1)
        for h in range(per_group):
            lanes = slice(h * 128, (h + 1) * 128)
            kv = kv_all[j, :, lanes]
            pair = nt(kv, both[h])
            pt = jnp.exp(jnp.where(ok, pair[:, :rows], MASKED) - logs[0, h : h + 1, :])
            dst = (pt * (pair[:, rows:] - balance[h])).astype(b16)
            dkv_all[j, :, lanes] += nn(jnp.concatenate([dst, pt.astype(b16)], axis=1), both[h])
            dq_acc[h] += tn(dst, kv)

    keep = lax.broadcasted_iota(jnp.int32, (rows, 128), 1) < 64
    for h in range(per_group):
        dq[0, :, h * 128 : (h + 1) * 128] = jnp.where(keep, dq_acc[h], 0.0).astype(b16)

    @pl.when(step == pl.num_programs(0) - 1)
    def _():
        if not ends:
            dkv_out[...] = dkv_all[...]
        else:
            for s in range(GROUPS):
                dkv_out[s] = dkv_all[block_of(sc, 0, s)]
                for entry, send in enumerate(dkv_send):
                    send[s] = dkv_all[block_of(sc, entry + 1, s)].astype(b16)


def lay_out(sc, pieces, own, par):
    z, c = sc[0], sc[1]
    ranks, half, width = own.shape[0], own.shape[1], own.shape[2] // 2
    for a in range(ranks):
        for side in range(2):
            at = pl.ds(pl.multiple_of((z ^ a) * 2 * half + side * half, 16), half)
            pieces[c, at, :] = own[a, :, side * width : (side + 1) * width]
            pieces[1 - c, at, :] = par[a, :, side * width : (side + 1) * width]


def group_rows(sc, s, size):
    return pl.ds(pl.multiple_of((sc[3] ^ s) * size, 16), size)


def out_kernel(sc, tok, a0, a1, a2, a3, own, par, vec, hat, rate, low, w):
    lay_out(sc, w, own, par)
    size = a0.shape[1]
    half = w.shape[2]
    sides = []
    for side in range(2):
        y = tok[:, side * half : (side + 1) * half].astype(f32)
        for s, a in enumerate((a0, a1, a2, a3)):
            y += nn(a[...], w[side, group_rows(sc, s, size), :])
        sides.append(y)
    resid = jnp.concatenate(sides, axis=1) + vec[2:3]
    h, r = normalised(resid)
    hat[...] = h
    rate[...] = jnp.broadcast_to(r, rate.shape)
    low[...] = (h * vec[3:4] + vec[4:5]).astype(b16)


def weights_of(sc, pieces, w):
    z = sc[0]
    rows = pieces.shape[1]
    for a in range(pieces.shape[0]):
        w[pl.ds(pl.multiple_of((z ^ a) * rows, 16), rows), :] = pieces[a]


def feed_kernel(sc, n_own, n_par, i0, i1, i2, i3, o0, o1, o2, o3, shift, act, slope, y_own, y_par, wi, wo):
    rows = n_own.shape[0]
    tokens = jnp.concatenate([n_own[...], n_par[...]], axis=0)
    total = jnp.zeros((2 * rows, n_own.shape[1]), f32)
    for s, (i, o) in enumerate(((i0, o0), (i1, o1), (i2, o2), (i3, o3))):
        weights_of(sc, i, wi.at[s])
        weights_of(sc, o, wo.at[s])
        inner = nn(tokens, wi[s]) + shift[s : s + 1, :]
        phi = 0.5 * (1.0 + lax.erf(inner * math.sqrt(0.5)))
        dens = jnp.exp(-0.5 * inner * inner) * (1.0 / math.sqrt(2.0 * math.pi))
        a = (inner * phi).astype(b16)
        act[s] = a
        slope[s] = (phi + inner * dens).astype(slope.dtype)
        total += nn(a, wo[s])
    y_own[...] = total[:rows]
    y_par[...] = total[rows:]


def close_kernel(sc, hat1, y_own, y_par, vec, cot, result, grad_two, low, sums):
    normed = hat1[...] * vec[3:4] + vec[4:5]
    h, r = normalised(normed + y_own[...] + y_par[...] + vec[5:6])
    result[...] = (h * vec[6:7] + vec[7:8]).astype(b16)
    c = cot[...].astype(f32)
    g = norm_back(c * vec[6:7], h, r)
    grad_two[...] = g
    g_low = g.astype(b16)
    low[...] = g_low
    sums[...] = jnp.zeros(sums.shape, f32)
    sums[0:1, :] = row_sum(g_low.astype(f32))
    sums[1:2, :] = row_sum(c * h)
    sums[2:3, :] = row_sum(c)


def feed_back_kernel(sc, g_own, g_par, i0, i1, i2, i3, o0, o1, o2, o3, slope, gi_out, y_own, y_par, gb, wi, wo):
    rows = g_own.shape[0]
    grads = jnp.concatenate([g_own[...], g_par[...]], axis=0)
    total = jnp.zeros((2 * rows, g_own.shape[1]), f32)
    for s, (i, o) in enumerate(((i0, o0), (i1, o1), (i2, o2), (i3, o3))):
        weights_of(sc, i, wi.at[s])
        weights_of(sc, o, wo.at[s])
        gi = (nt(grads, wo[s]) * slope[s].astype(f32)).astype(b16)
        gi_out[s] = gi
        gb[s : s + 1, :] = row_sum(gi.astype(f32))
        total += nt(gi, wi[s])
    y_own[...] = total[:rows]
    y_par[...] = total[rows:]


def feed_grads(sc, s, n_own, n_par, g_own, g_par, act, gi, gb, ranks):
    tokens = jnp.concatenate([n_own[...], n_par[...]], axis=0)
    grads = jnp.concatenate([g_own[...], g_par[...]], axis=0)
    inner = tn(tokens, gi[s])
    outer = tn(act[s], grads)
    half = inner.shape[0] // (2 * ranks)
    piece = outer.shape[0] // ranks
    d = outer.shape[1]
    foot = jnp.concatenate([gb[s : s + 1, :], jnp.zeros((1, d - gb.shape[1]), f32)], axis=1)
    foot = jnp.concatenate([foot, jnp.zeros((7, d), f32)], axis=0)
    ins, outs = [], []
    for k in range(ranks):
        top = inner[2 * k * half : (2 * k + 1) * half]
        ins.append(jnp.concatenate([top, inner[(2 * k + 1) * half : (2 * k + 2) * half]], axis=1))
        outs.append(jnp.concatenate([outer[k * piece : (k + 1) * piece], foot], axis=0))
    return ins, outs


def feed_weights_far_kernel(sc, n_own, n_par, g_own, g_par, act, gi, gb, i_out, o_out):
    ins, outs = feed_grads(sc, 3, n_own, n_par, g_own, g_par, act, gi, gb, i_out.shape[0])
    for k, (i, o) in enumerate(zip(ins, outs)):
        i_out[k] = i.astype(b16)
        o_out[k] = o.astype(b16)


def feed_weights_kernel(sc, n_own, n_par, g_own, g_par, act, gi, gb, i_in, o_in, p0, p1, p2):
    ranks, half = i_in.shape[0], i_in.shape[1]
    for s, out in ((1, p1), (2, p2), (0, p0)):
        ins, outs = feed_grads(sc, s, n_own, n_par, g_own, g_par, act, gi, gb, ranks)
        for k, (i, o) in enumerate(zip(ins, outs)):
            if s == 2:
                i = i + i_in[k].astype(f32)
            if s == 1:
                o = o + o_in[k].astype(f32)
            out[k, :half] = i.astype(b16)
            out[k, half:] = o.astype(b16)


def first_back_kernel(sc, grad_two, y_own, y_par, hat, rate, vec, own, par, grad_one, low, b0, b1, b2, b3, sums, w):
    lay_out(sc, w, own, par)
    gn = grad_two[...] + y_own[...] + y_par[...]
    h = hat[...]
    g = norm_back(gn * vec[3:4], h, rate[:, 0:1])
    grad_one[...] = g
    g_low = g.astype(b16)
    low[...] = g_low
    sums[...] = jnp.zeros(sums.shape, f32)
    sums[0:1, :] = row_sum(g_low.astype(f32))
    sums[1:2, :] = row_sum(gn * h)
    sums[2:3, :] = row_sum(gn)
    half = w.shape[2]
    lo, hi = g_low[:, :half], g_low[:, half:]
    for s, b in enumerate((b0, b1, b2, b3)):
        at = group_rows(sc, s, b.shape[1])
        b[...] = (nt(lo, w[0, at, :]) + nt(hi, w[1, at, :])).astype(b16)


def out_weights_kernel(sc, low, a0, a1, a2, a3, gw_own, gw_par, both):
    c = sc[1]
    ranks, half = gw_own.shape[0], gw_own.shape[1]
    width = low.shape[1] // 2
    lo, hi = low[:, :width], low[:, width:]
    mine = jnp.where(c == 0, lo, hi)
    other = jnp.where(c == 0, hi, lo)
    for s, a in enumerate((a0, a1, a2, a3)):
        at = group_rows(sc, s, a.shape[1])
        both[0, at, :] = tn(a[...], mine).astype(b16)
        both[1, at, :] = tn(a[...], other).astype(b16)
    for k in range(ranks):
        for side in range(2):
            rows = slice((2 * k + side) * half, (2 * k + side + 1) * half)
            gw_own[k, :, side * width : (side + 1) * width] = both[0, rows, :]
            gw_par[k, :, side * width : (side + 1) * width] = both[1, rows, :]


def finish_feed_kernel(sc, near, far, d_inner, d_outer, d_shift, d_out):
    z, c, g = sc[0], sc[1], sc[3]
    half = d_inner.shape[0] // 2
    piece = near.shape[1] - 8 - 2 * half
    ranks = d_inner.shape[1] // (2 * GROUPS * piece)
    width = d_out.shape[1] // 2
    tops, feet = [], []
    for core in range(2):
        total = jnp.zeros((half, 2 * width), f32)
        for k in range(GROUPS):
            at = g ^ k
            block = jnp.where(core == c, near[at], far[at]).astype(f32)
            total += block[half + piece + 8 :]
            row = (core * GROUPS + k) * piece
            d_outer[row : row + piece, :] = block[half : half + piece]
            tops.append(block[:half])
            foot = block[half + piece : half + piece + 1]
            shift = jnp.zeros((1, piece), f32)
            for y in range(ranks):
                shift = jnp.where(z == y, foot[:, y * piece : (y + 1) * piece], shift)
            feet.append(shift)
        for side in range(2):
            at = slice(side * half, (side + 1) * half)
            d_out[at, core * width : (core + 1) * width] = total[:, side * width : (side + 1) * width]
    d_shift[...] = jnp.concatenate(feet, axis=1)
    wide = ranks * piece
    for y in range(ranks):
        for side in range(2):
            low = side * wide + y * piece
            width = 2 * GROUPS * piece
            d_inner[side * half : (side + 1) * half, y * width : (y + 1) * width] = jnp.concatenate(
                [t[:, low : low + piece] for t in tops], axis=1
            )


def finish_kernel(sc, near, far, d_query, d_key, d_value, vec):
    z, c, g = sc[0], sc[1], sc[3]
    dz, d = d_query.shape
    half = dz // 2
    hd = d // HEADS
    per_group = HEADS // GROUPS
    wide = 2 * per_group * hd
    rows = [[None] * GROUPS, [None] * GROUPS]
    total = jnp.zeros((8, d), f32)
    for core in range(2):
        queries, keys, values = [], [], []
        for k in range(GROUPS):
            block = jnp.where(core == c, near[g ^ k], far[g ^ k]).astype(f32)
            for h in range(per_group):
                queries.append(block[:half, 2 * h * hd : (2 * h + 1) * hd] * 0.125)
                keys.append(block[:half, wide + 2 * h * hd : wide + (2 * h + 1) * hd])
                values.append(block[:half, wide + (2 * h + 1) * hd : wide + (2 * h + 2) * hd])
            total += block[half:]
            rows[core][k] = block[half : half + 1]
        at = slice(core * half, (core + 1) * half)
        d_query[at] = jnp.concatenate(queries, axis=1)
        d_key[at] = jnp.concatenate(keys, axis=1)
        d_value[at] = jnp.concatenate(values, axis=1)
    queries, values = [], []
    for k in range(GROUPS):
        row = rows[0][k] + rows[1][k]
        for h in range(per_group):
            queries.append(row[:, 2 * h * hd : (2 * h + 1) * hd] * 0.125)
            values.append(row[:, wide + (2 * h + 1) * hd : wide + (2 * h + 2) * hd])
    full = jnp.concatenate([jnp.concatenate(queries, axis=1), jnp.concatenate(values, axis=1), total[1:7]], axis=0)
    picked = jnp.zeros((8, dz), f32)
    for k in range(d // dz):
        picked = jnp.where(z == k, full[:, k * dz : (k + 1) * dz], picked)
    vec[...] = picked


def per_device(
    tokens,
    segments,
    w_query,
    b_query,
    w_key,
    w_value,
    b_value,
    w_out,
    b_out,
    gain_attention,
    bias_attention,
    w_inner,
    b_inner,
    w_outer,
    b_outer,
    gain_feed,
    bias_feed,
    cotangent,
):
    n = lax.axis_size("ctx")
    ranks = lax.axis_size("fsdp")
    place = lax.axis_index("ctx")
    z = lax.axis_index("fsdp")
    rows, d = tokens.shape[1], tokens.shape[2]
    ff = w_inner.shape[1]
    c, chip = place & 1, place >> 1
    g, r = chip % GROUPS, chip // GROUPS
    sets = n // GROUPS
    rank = r * 2 + c
    per_group = HEADS // GROUPS
    hd = d // HEADS
    gw = per_group * hd
    dz, fz = d // ranks, ff // ranks
    half = dz // 2
    piece = fz // (2 * GROUPS)
    cols = ranks * piece
    wide = per_group * 2 * hd
    sc = jnp.stack([z, c, rank, g]).astype(jnp.int32)
    X, Y, CORE = 2, 4, 1
    flips = [(t & 1) | ((t >> 1) * 2 * GROUPS) for t in range(sets)]

    def over_z(x):
        return [x] + [swap(x, "fsdp", a) for a in range(1, ranks)]

    def over_group(x):
        return [x] + [swap(x, "ctx", s << 1) for s in range(1, GROUPS)]

    def spread(kernel, operands, size, name):
        return whole_call(
            kernel,
            [shape(size, f32)] + [shape(size, b16)] * (ranks - 1),
            1 + len(operands),
            name=name,
        )(sc, *operands)

    tok = tokens[0]
    toks = over_group(tok)

    vectors = (b_query, b_value, b_out, gain_attention, bias_attention, b_outer, gain_feed, bias_feed, b_inner)
    (first,) = whole_call(
        pack_first_kernel, [shape((half + 8, d), b16)], 13, name="pack_first"
    )(sc, w_query, w_key, w_value, *vectors)
    got1, got2 = swap(first, "fsdp", 1), swap(first, "fsdp", 2)
    first_all = jnp.stack([first, got1, got2] + [swap(after(first, got1), "fsdp", a) for a in range(3, ranks)])
    proj_own = first_all[:, :half]
    proj_par = swap(proj_own, "ctx", CORE)
    vec, shift_qkv, shift_inner = whole_call(
        vectors_kernel,
        [shape((8, d), f32), shape((1, 2 * wide), f32), shape((GROUPS, cols), f32)],
        2,
        [pltpu.VMEM((8, d), f32), pltpu.VMEM((2 * GROUPS, cols), f32)],
        name="vectors",
    )(sc, first_all[:, half:])

    q, kv, w_qkv = whole_call(
        project_kernel,
        [shape((GROUPS, rows, wide), b16), shape((GROUPS, rows, wide), b16), shape((d, 2 * wide), b16)],
        8,
        name="project",
    )(sc, *toks, proj_own, proj_par, shift_qkv)
    wi, second = whole_call(
        pack_feed_kernel, [shape((dz, cols), b16), shape((piece + half, d), b16)], 4, name="pack_feed"
    )(sc, after(w_inner, first), w_outer, w_out)
    wi_parts = over_z(after(wi, got2))
    kvs = [kv] + [swap(after(kv, *wi_parts), "ctx", f) for f in flips[1:]]
    wo_parts = over_z(after(second, q))

    seg = segments[0].reshape(n, rows)
    begin, end = seg[:, 0], seg[:, -1]
    span = jnp.stack(
        [
            jnp.sum((end[None, :] < begin[:, None]).astype(jnp.int32), axis=1),
            jnp.sum((begin[None, :] <= end[:, None]).astype(jnp.int32), axis=1),
        ],
        axis=1,
    )
    seg_rows = seg.reshape(n, 1, rows)
    seg_cols = jnp.broadcast_to(seg[:, :, None], (n, rows, 128))

    smem = pl.BlockSpec(memory_space=pltpu.SMEM)

    def fixed(dims):
        return pl.BlockSpec(dims, lambda s: (0,) * len(dims))

    def stepped(dims):
        return pl.BlockSpec((1,) + dims, lambda s: (s,) + (0,) * len(dims))

    kv_specs = [fixed((GROUPS, rows, wide))] * sets

    def attend(q, start, count):
        def falling(dims):
            return pl.BlockSpec((1,) + dims, lambda s: (start - s,) + (0,) * len(dims))

        return pl.pallas_call(
            functools.partial(attend_kernel, start),
            grid=(count,),
            in_specs=[smem, smem, falling((rows, wide)), fixed((n, 1, rows)), fixed((n, rows, 128))] + kv_specs,
            out_specs=[stepped((rows, gw)), stepped((rows, gw)), stepped((8, rows))],
            out_shape=[shape((count, rows, gw), f32), shape((count, rows, gw), b16), shape((count, 8, rows), f32)],
            scratch_shapes=[
                pltpu.VMEM((n, rows, wide), b16),
                pltpu.VMEM((per_group, n, rows, rows), f32),
                pltpu.VMEM((per_group, rows, 128), f32),
                pltpu.VMEM((per_group, rows, 128), f32),
            ],
            name="attend",
            cost_estimate=cost("attend"),
        )(sc, span, q, seg_rows, seg_cols, *kvs)

    wi_z = jnp.stack(wi_parts)
    wi1, wi2 = swap(wi_z, "ctx", X), swap(after(wi_z, *kvs), "ctx", Y)
    seg_rows = after(seg_rows, wi_z)
    mixed_far, low_far, logs_far = attend(q, GROUPS - 1, 2)
    wi3 = swap(after(wi1, low_far, wi2), "ctx", Y)
    mixed_near, low_near, logs_near = attend(after(q, low_far), 1, 2)
    wo_parts = after(tuple(wo_parts), low_near, wi3)
    wo_z, wout_own = whole_call(
        split_second_kernel,
        [shape((ranks, piece, d), b16), shape((ranks, half, d), b16)],
        1 + ranks,
        name="split_second",
    )(sc, *wo_parts)
    wo1, wo2 = swap(wo_z, "ctx", X), swap(wo_z, "ctx", Y)
    wo3 = swap(wo2, "ctx", X)
    atts = [low_near[1], swap(low_near[0], "ctx", X), swap(low_far[1], "ctx", Y), swap(low_far[0], "ctx", X + Y)]
    wout_par = swap(after(wout_own, atts[3]), "ctx", CORE)
    wis, wos = (wi_z, wi1, wi2, wi3), (wo_z, wo1, wo2, wo3)

    hat1, rate1, low = whole_call(
        out_kernel,
        [shape((rows, d), f32), shape((rows, 128), f32), shape((rows, d), b16)],
        9,
        [pltpu.VMEM((2, d, d // 2), b16)],
        name="out",
    )(sc, tok, *atts, wout_own, wout_par, vec)
    low_par = swap(low, "ctx", CORE)

    scratch = [pltpu.VMEM((GROUPS, d, cols), b16), pltpu.VMEM((GROUPS, cols, d), b16)]
    hidden = (GROUPS, 2 * rows, cols)
    act, slope, y_own, y_send = whole_call(
        feed_kernel,
        [shape(hidden, b16), shape(hidden, b16), shape((rows, d), f32), shape((rows, d), f32)],
        12,
        scratch,
        name="feed",
    )(sc, low, low_par, *wis, *wos, shift_inner)
    y_par = swap(y_send, "ctx", CORE)

    result, grad_two, gol, sums_two = whole_call(
        close_kernel,
        [shape((rows, d), b16), shape((rows, d), f32), shape((rows, d), b16), shape((8, d), f32)],
        6,
        name="close",
    )(sc, hat1, y_own, y_par, vec, cotangent[0])
    gol_par = swap(gol, "ctx", CORE)

    gi, gn_own, gn_send, gb_inner = whole_call(
        feed_back_kernel,
        [shape(hidden, b16), shape((rows, d), f32), shape((rows, d), f32), shape((GROUPS, cols), f32)],
        12,
        scratch,
        name="feed_back",
    )(sc, gol, gol_par, *wis, *wos, slope)
    gn_par = swap(gn_send, "ctx", CORE)

    grad_one, gbl, *ga, sums_one = whole_call(
        first_back_kernel,
        [shape((rows, d), f32), shape((rows, d), b16)] + [shape((rows, gw), b16)] * GROUPS + [shape((8, d), f32)],
        9,
        [pltpu.VMEM((2, d, d // 2), b16)],
        name="first_back",
    )(sc, grad_two, gn_own, gn_par, hat1, rate1, vec, wout_own, wout_par)
    grads_att = [ga[0]] + [swap(ga[s], "ctx", s << 1) for s in range(1, GROUPS)]

    far_i, far_o = whole_call(
        feed_weights_far_kernel,
        [shape((ranks, half, d), b16), shape((ranks, piece + 8, d), b16)],
        8,
        name="feed_weights_far",
    )(sc, low, low_par, gol, gol_par, act, gi, after(gb_inner, gbl))
    in_i, in_o = swap(far_i, "ctx", X), swap(far_o, "ctx", Y)

    gwout_own, gwout_send = whole_call(
        out_weights_kernel,
        [shape((ranks, half, d), b16)] * 2,
        6,
        [pltpu.VMEM((2, d, d // 2), b16)],
        name="out_weights",
    )(sc, gbl, *atts)
    out_own, *out_sends = spread(
        spread_out_kernel, (gwout_own, swap(gwout_send, "ctx", CORE)), (half, d), "spread_out"
    )
    out_got = [swap(send, "fsdp", a + 1) for a, send in enumerate(out_sends)]

    def attend_back(start, count, grads, mixed, logs, before, ends):
        def falling(dims):
            return pl.BlockSpec((1,) + dims, lambda s: (start - s,) + (0,) * len(dims))

        begins = not before
        whole_kv = [shape((GROUPS, rows, wide), f32)] + [shape((GROUPS, rows, wide), b16)] * (sets - 1)
        return pl.pallas_call(
            functools.partial(attend_back_kernel, (start, count, begins, ends)),
            grid=(count,),
            in_specs=[smem, smem, falling((rows, wide)), fixed((n, 1, rows)), fixed((n, rows, 128))]
            + [fixed((rows, gw))] * count
            + [stepped((rows, gw)), stepped((8, rows))]
            + kv_specs
            + [fixed((n, rows, wide))] * len(before),
            out_specs=[stepped((rows, wide))] + (kv_specs if ends else [fixed((n, rows, wide))]),
            out_shape=[shape((count, rows, wide), b16)] + (whole_kv if ends else [shape((n, rows, wide), f32)]),
            scratch_shapes=[
                pltpu.VMEM((n, rows, wide), b16),
                pltpu.VMEM((n, rows, wide), f32),
                pltpu.VMEM((per_group, rows, 128), f32),
                pltpu.VMEM((per_group, 2 * rows, 128), b16),
            ],
            name="attend_back",
            cost_estimate=cost("attend_back"),
        )(sc, span, q, seg_rows, seg_cols, *grads, mixed, logs, *kvs, *before)

    dq_far, dkv_part = attend_back(GROUPS - 1, 2, (grads_att[3], after(grads_att[2], grads_att[1])), mixed_far, logs_far, (), False)
    packs = whole_call(
        feed_weights_kernel,
        [shape((ranks, half + piece + 8, d), b16)] * 3,
        10,
        name="feed_weights",
    )(sc, low, low_par, gol, gol_par, act, gi, after(gb_inner, dq_far, *out_got), in_i, in_o)
    pack0, pack1, pack2 = packs
    pack1, pack2 = swap(pack1, "ctx", X), swap(pack2, "ctx", Y)

    dq_near, dkv_own, *dkv_send = attend_back(
        1, 2, (grads_att[1], grads_att[0]), mixed_near, after(logs_near, pack0), (dkv_part,), True
    )
    dkv_send = list(after(tuple(dkv_send), pack1, pack2))
    pack0, pack1, pack2, out_got = after((pack0, pack1, pack2, tuple(out_got)), dq_near)
    feed_own, *feed_sends = spread(
        spread_feed_kernel, (pack0, pack1, pack2), (half + piece + 8, d), "spread_feed"
    )
    feed_got = [swap(send, "fsdp", a + 1) for a, send in enumerate(feed_sends)]
    dkv_in = swap(dkv_send[0], "ctx", flips[1])
    for t in range(2, sets):
        dkv_own = dkv_own + swap(dkv_send[t - 1], "ctx", flips[t]).astype(f32)

    def all_sum(x):
        total = x
        for t in range(1, sets // 2):
            total = total + swap(x, "ctx", t * 2 * GROUPS)
        return total

    keep, give, sums, grads_qkv = whole_call(
        project_weights_kernel,
        [
            shape((ranks, half, 2 * wide), f32),
            shape((ranks, half, 2 * wide), b16),
            shape((8, d), f32),
            shape((GROUPS, rows, 2 * wide), b16),
        ],
        11,
        [pltpu.VMEM((d, 2 * wide), f32)],
        name="project_weights",
    )(sc, *toks, dq_far, dq_near, dkv_own, dkv_in, sums_one, sums_two)
    got = swap(give, "ctx", CORE)

    qkv_own, *qkv_sends = spread(spread_kernel, (keep, got, sums), (half + 8, 2 * wide), "spread")
    qkv_got = [swap(send, "fsdp", a + 1) for a, send in enumerate(qkv_sends)]

    dx_own, *dxs = whole_call(
        project_back_kernel,
        [shape((rows, d), f32)] + [shape((rows, d), b16)] * (GROUPS - 1),
        4,
        name="project_back",
    )(sc, grads_qkv, w_qkv, after(grad_one, qkv_own))
    grad_input = dx_own
    for s in range(1, GROUPS):
        grad_input = grad_input + swap(dxs[s - 1], "ctx", s << 1).astype(f32)

    def total_of(own, got):
        total = own
        for part in got:
            total = total + part.astype(f32)
        return all_sum(total).astype(b16)

    def everywhere(x):
        pieces = jnp.stack(over_group(x))
        return pieces, swap(pieces, "ctx", CORE)

    feed_got = after(tuple(feed_got), qkv_own)
    feed_near, feed_far = everywhere(
        jnp.concatenate([total_of(feed_own, feed_got), total_of(out_own, out_got)], axis=0)
    )
    d_inner, d_outer, d_shift, d_out = whole_call(
        finish_feed_kernel,
        [shape((dz, ff), f32), shape((fz, d), f32), shape((1, fz), f32), shape((dz, d), f32)],
        3,
        name="finish_feed",
    )(sc, feed_near, feed_far)
    d_query, d_key, d_value, vs = whole_call(
        finish_kernel,
        [shape((dz, d), f32)] * 3 + [shape((8, dz), f32)],
        3,
        name="finish",
    )(sc, *everywhere(total_of(qkv_own, qkv_got)))

    return (
        result[None],
        grad_input[None],
        d_query,
        vs[0],
        d_key,
        d_value,
        vs[1],
        d_out,
        vs[2],
        vs[3],
        vs[4],
        d_inner,
        d_shift[0],
        d_outer,
        vs[5],
        vs[6],
        vs[7],
    )


def solution(mesh):
    rows = P("fsdp", "ctx", None)
    matrix = P("fsdp", None)
    vector = P("fsdp")
    return jax.shard_map(
        per_device,
        mesh=mesh,
        in_specs=(rows, matrix, matrix, vector, matrix, matrix, vector, matrix, vector, vector, vector)
        + (matrix, vector, matrix, vector, vector, vector, rows),
        out_specs=(rows, rows, matrix, vector, matrix, matrix, vector, matrix, vector, vector, vector)
        + (matrix, vector, matrix, vector, vector, vector),
        check_vma=False,
    )
```

time: 459 us -> 341 us (0.74)
  local copies, waits for them, and re-layouts: 70.8 us -> 14.7 us
  other arithmetic: 44.8 us -> 6.41 us
  starting transfers between devices: 73 us -> 55.6 us
    ppermute x74 -> x58, starting transfers between devices: 73 us -> 55.6 us  [swap(): lax.ppermute(x, axis, [(i, i ^ flip) for i in range(lax.axis_size(axis))])]
    convert_element_type x5 -> x0, local copies, waits for them, and re-layouts: 13.8 us -> none  [the longest x2 7.22 us: per_device(): qkv.transpose(0, 2, 1, 3).reshape(dz, GROUPS, 2, per_group, 2, hd)]
    gather x13 -> x0, local copies, waits for them, and re-layouts: 13.4 us -> none  [the longest x8 10.9 us: ordered(): return jnp.take(jnp.take(x, core_order, axis=0), group_order, axis=1)]
    another operation x12 -> x2, other arithmetic: 13.1 us -> 0.18 us  [the longest x1 0.09 us: per_device(): wi_z = jnp.stack(wi_parts)]
    reshape x15 -> x0, local copies, waits for them, and re-layouts: 9.55 us -> none  [the longest x6 4.69 us: per_device(): vec = [vec_all[:, k * dz:(k + 1) * dz].reshape(1, d) for k in range(8)]]
    convert_element_type x14 -> x3, other arithmetic: 8.64 us -> 1.37 us  [total_of(): return all_sum(total).astype(b16)]
    another operation x13 -> x0, local copies, waits for them, and re-layouts: 5.27 us -> none  [the longest x6 3.42 us: per_device(): v.reshape(ranks, dz)]
    unnamed x163 -> x83, local copies, waits for them, and re-layouts: 13.1 us -> 9.32 us
  transfers between devices with their start and end apart: 74 -> 58, of which waited for: 27 -> 24; matrix products, arithmetic and copies ran while one was open for 16% -> 3% of each run, Pallas kernels for 25% -> 31%
where the time goes in v2:
time: 341 us; the launch traced here: 338 us
  Pallas kernels  150 us (44%)
  waiting for transfers between devices  111 us (33%)
  starting transfers between devices  55.6 us (16%)
  local copies, waits for them, and re-layouts  14.7 us (4%)
  other arithmetic  6.41 us (2%)
    ppermute x58, waiting for transfers between devices, swap(): lax.ppermute(x, axis, [(i, i ^ flip) for i in range(lax.axis_size(axis))])  111 us
    ppermute x58, starting transfers between devices, swap(): lax.ppermute(x, axis, [(i, i ^ flip) for i in range(lax.axis_size(axis))])  55.6 us
    pallas_call x2, Pallas kernels, attend_back(): pl.pallas_call(functools.partial(attend_back_kernel, (start, count, begin...  43.3 us
    pallas_call x2, Pallas kernels, attend(): pl.pallas_call(functools.partial(attend_kernel, start), grid=(count,), in...  24.4 us
    unnamed x83, local copies, waits for them, and re-layouts  9.32 us
    pallas_call x1, Pallas kernels, per_device(): whole_call(feed_kernel, [shape(hidden, b16), shape(hidden, b16), shape((r...  8.39 us
    pallas_call x1, Pallas kernels, per_device(): whole_call(feed_back_kernel, [shape(hidden, b16), shape((rows, d), f32),...  8.01 us
    pallas_call x3, Pallas kernels, spread(): whole_call(kernel, [shape(size, f32)] + [shape(size, b16)] * (ranks - 1),...  7.97 us
  transfers between devices with their start and end apart: 58, of which 24 were waited for; matrix products, arithmetic and copies ran while one was open for 3% of the time, Pallas kernels for 31%

profile of v2, /device:TPU:14, one launch (start us, length us, event | category | flops | bytes accessed | tf_op | source)
XLA Modules:
  0.0 338.4 jit_solution(8269764166004513164)
XLA Ops:
  15.3 9.3 %collective-permute-done.5 = bf16[104,768]{1,0:T(8,128)(2,1)S(1)} collective-permute-done((bf16[104,768]{1,0:T(8,128)(2,1)}, bf16[104,768]{1,0:T(8,128)(2,1)S(1)}, u32[]{:S(2)}, u32[]{:S(2)}) %collective-permute-start.5) | collective-permute-done | bytes 159776 | tf_op jit(solution)/shard_map/ppermute | solution.py:20
  27.6 3.8 %collective-permute-start.7 = (bf16[192,384]{1,0:T(8,128)(2,1)S(1)}, bf16[192,384]{1,0:T(8,128)(2,1)S(1)}, u32[]{:S(2)}, u32[]{:S(2)}) collective-permute-start(bf16[192,384]{1,0:T(8,128)(2,1)S(1)} %copy-done.10), channel_id=1, source_target_pairs={{0,1},{1,0},{2,3},{3,2},{4,5},{5,4},{6,7},{7,6},{8,9},{9,8},{10,11... | collective-permute-start | bytes 442376 | tf_op jit(solution)/shard_map/ppermute | solution.py:20
  32.3 4.7 %project.1 = (bf16[4,256,384]{2,1,0:T(8,128)(2,1)}, bf16[4,256,384]{2,1,0:T(8,128)(2,1)}, bf16[768,768]{1,0:T(8,128)(2,1)}) custom-call(s32[4]{0:T(128)} %pad_add_fusion.1.sc, bf16[256,768]{1,0:T(8,128)(2,1)} %bitcast.83, bf16[256,768]{1,0:T(8,128)(2,1)} %copy-done.30, bf16[256,768]{1,0:T(8,128)(2,1)} %copy-done.29, bf16[256,768]{1,0:T(8,128)(2,1)} %copy-done.28, ...), custom_call_target="tpu_custom_call" | custom-call | flops 49999998976 | bytes 1000000 | tf_op jit(solution)/shard_map/project/pallas_call | solution.py:678
  41.7 3.7 %collective-permute-start.15 = (bf16[192,768]{1,0:T(8,128)(2,1)}, bf16[192,768]{1,0:T(8,128)(2,1)}, u32[]{:S(2)}, u32[]{:S(2)}) collective-permute-start(bf16[192,768]{1,0:T(8,128)(2,1)} %get-tuple-element.140.refs_0_), channel_id=1, source_target_pairs={{0,2},{1,3},{2,0},{3,1},{4,6},{5,7},{6,4},{7,5},{8,10},{9,11},{10,... | collective-permute-start | bytes 884744 | tf_op jit(solution)/shard_map/ppermute | solution.py:20
  47.3 11.9 %attend.2 = (f32[2,256,192]{2,1,0:T(8,128)}, bf16[2,256,192]{2,1,0:T(8,128)(2,1)}, f32[2,8,256]{2,1,0:T(8,128)}) custom-call(s32[4]{0:T(128)} %pad_add_fusion.1.sc, s32[8,2]{1,0:T(8,128)} %copy.48.span, bf16[4,256,384]{2,1,0:T(8,128)(2,1)} %get-tuple-element.134.q, s32[8,1,256]{2,1,0:T(1,128)} %bitcast.66, s32[8,256,128]{2,1,0:T(8,128)} %broadcast_in_dim.11.seg_cols, ...), custom_call_target="tpu_custom_call" | custom-call | flops 109999996928 | bytes 1000000 | tf_op jit(solution)/shard_map/attend/pallas_call | solution.py:717
  60.2 3.1 collective-permute-start.13
  63.3 12.6 %attend.3 = (f32[2,256,192]{2,1,0:T(8,128)}, bf16[2,256,192]{2,1,0:T(8,128)(2,1)}, f32[2,8,256]{2,1,0:T(8,128)}) custom-call(s32[4]{0:T(128)} %pad_add_fusion.1.sc, s32[8,2]{1,0:T(8,128)} %copy.48.span, bf16[4,256,384]{2,1,0:T(8,128)(2,1)} %get-tuple-element.134.q, s32[8,1,256]{2,1,0:T(1,128)} %bitcast.67, s32[8,256,128]{2,1,0:T(8,128)} %broadcast_in_dim.11.seg_cols, ...), custom_call_target="tpu_custom_call" | custom-call | flops 109999996928 | bytes 1000000 | tf_op jit(solution)/shard_map/attend/pallas_call | solution.py:717
  85.9 11.2 %collective-permute-done.23.o2 = bf16[4,96,768]{2,1,0:T(8,128)(2,1)S(1)} collective-permute-done((bf16[4,96,768]{2,1,0:T(8,128)(2,1)}, bf16[4,96,768]{2,1,0:T(8,128)(2,1)S(1)}, u32[]{:S(2)}, u32[]{:S(2)}) %collective-permute-start.23) | collective-permute-done | bytes 589856 | tf_op jit(solution)/shard_map/ppermute | solution.py:20
  99.4 3.7 %out.1 = (f32[256,768]{1,0:T(8,128)}, f32[256,128]{1,0:T(8,128)}, bf16[256,768]{1,0:T(8,128)(2,1)}) custom-call(s32[4]{0:T(128)} %pad_add_fusion.1.sc, bf16[256,768]{1,0:T(8,128)(2,1)} %bitcast.84, bf16[256,192]{1,0:T(8,128)(2,1)} %get-tuple-element.238.a0, bf16[256,192]{1,0:T(8,128)(2,1)} %copy-done.36, bf16[256,192]{1,0:T(8,128)(2,1)} %copy-done.35, ...), custom_call_target="tpu_custom_call" | custom-call | flops 40000000000 | bytes 1000000 | tf_op jit(solution)/shard_map/out/pallas_call | solution.py:752
  105.1 9.7 %collective-permute-done.24.o3 = bf16[4,96,768]{2,1,0:T(8,128)(2,1)S(1)} collective-permute-done((bf16[4,96,768]{2,1,0:T(8,128)(2,1)S(1)}, bf16[4,96,768]{2,1,0:T(8,128)(2,1)S(1)}, u32[]{:S(2)}, u32[]{:S(2)}) %collective-permute-start.24) | collective-permute-done | bytes 589856 | tf_op jit(solution)/shard_map/ppermute | solution.py:20
  115.5 8.4 %feed.1 = (bf16[4,512,384]{2,1,0:T(8,128)(2,1)}, bf16[4,512,384]{2,1,0:T(8,128)(2,1)}, f32[256,768]{1,0:T(8,128)}, f32[256,768]{1,0:T(8,128)}) custom-call(s32[4]{0:T(128)} %pad_add_fusion.1.sc, bf16[256,768]{1,0:T(8,128)(2,1)} %get-tuple-element.148.n_own, bf16[256,768]{1,0:T(8,128)(2,1)} %copy-done.31, bf16[4,192,384]{2,1,0:T(8,128)(2,1)} %copy-done.5, ...), custom_call_target="tpu_custom_call" | custom-call | flops 80000000000 | bytes 1000000 | tf_op jit(solution)/shard_map/feed/pallas_call | solution.py:763
  127.3 3.5 %close.1 = (bf16[256,768]{1,0:T(8,128)(2,1)}, f32[256,768]{1,0:T(8,128)}, bf16[256,768]{1,0:T(8,128)(2,1)}, f32[8,768]{1,0:T(8,128)}) custom-call(s32[4]{0:T(128)} %pad_add_fusion.1.sc, f32[256,768]{1,0:T(8,128)} %get-tuple-element.147.hat1.hat, f32[256,768]{1,0:T(8,128)} %get-tuple-element.151.y_own, f32[256,768]{1,0:T(8,128)} %copy-done.15, ...), custom_call_target="tpu_custom_call" | custom-call | flops 40000000000 | bytes 1000000 | tf_op jit(solution)/shard_map/close/pallas_call | solution.py:772
  133.5 8.0 %feed_back.1 = (bf16[4,512,384]{2,1,0:T(8,128)(2,1)}, f32[256,768]{1,0:T(8,128)}, f32[256,768]{1,0:T(8,128)}, f32[4,384]{1,0:T(4,128)}) custom-call(s32[4]{0:T(128)} %pad_add_fusion.1.sc, bf16[256,768]{1,0:T(8,128)(2,1)} %get-tuple-element.155.g_own, bf16[256,768]{1,0:T(8,128)(2,1)} %copy-done.32, bf16[4,192,384]{2,1,0:T(8,128)(2,1)} %copy-done.5, ...), custom_call_target="tpu_custom_call" | custom-call | flops 80000000000 | bytes 1000000 | tf_op jit(solution)/shard_map/feed_back/pallas_call | solution.py:780
  144.9 4.3 %first_back.1 = (f32[256,768]{1,0:T(8,128)}, bf16[256,768]{1,0:T(8,128)(2,1)}, bf16[256,192]{1,0:T(8,128)(2,1)}, bf16[256,192]{1,0:T(8,128)(2,1)}, bf16[256,192]...) custom-call(s32[4]{0:T(128)} %pad_add_fusion.1.sc, f32[256,768]{1,0:T(8,128)} %get-tuple-element.154.grad_two, ...), custom_call_target="tpu_custom_call" | custom-call | flops 40000000000 | bytes 1000000 | tf_op jit(solution)/shard_map/first_back/pallas_call | solution.py:789
  152.7 2.9 out_weights.1
  155.6 4.4 %feed_weights_far.1 = (bf16[4,96,768]{2,1,0:T(8,128)(2,1)}, bf16[4,104,768]{2,1,0:T(8,128)(2,1)}) custom-call(s32[4]{0:T(128)} %pad_add_fusion.1.sc, bf16[256,768]{1,0:T(8,128)(2,1)} %get-tuple-element.148.n_own, bf16[256,768]{1,0:T(8,128)(2,1)} %copy-done.31, bf16[256,768]{1,0:T(8,128)(2,1)} %get-tuple-element.155.g_own, bf16[256,768]{1,0:T(8,128)(2,1)} %copy-done.32, ...), custom_call_target="tpu_custom_call" | custom-call | flops 40000000000 | bytes 1000000 | tf_op jit(solution)/shard_map/feed_weights_far/pallas_call | solution.py:798
  167.5 20.7 %attend_back.2 = (bf16[2,256,384]{2,1,0:T(8,128)(2,1)}, f32[8,256,384]{2,1,0:T(8,128)}) custom-call(s32[4]{0:T(128)} %pad_add_fusion.1.sc, s32[8,2]{1,0:T(8,128)} %copy.48.span, bf16[4,256,384]{2,1,0:T(8,128)(2,1)} %get-tuple-element.134.q, s32[8,1,256]{2,1,0:T(1,128)} %bitcast.68, s32[8,256,128]{2,1,0:T(8,128)} %broadcast_in_dim.11.seg_cols, ...), custom_call_target="tpu_custom_call" | custom-call | flops 219999993856 | bytes 1000000 | tf_op jit(solution)/shard_map/attend_back/pallas_call | solution.py:824
  188.3 6.9 %feed_weights.1 = (bf16[4,200,768]{2,1,0:T(8,128)(2,1)}, bf16[4,200,768]{2,1,0:T(8,128)(2,1)}, bf16[4,200,768]{2,1,0:T(8,128)(2,1)}) custom-call(s32[4]{0:T(128)} %pad_add_fusion.1.sc, bf16[256,768]{1,0:T(8,128)(2,1)} %get-tuple-element.148.n_own, bf16[256,768]{1,0:T(8,128)(2,1)} %copy-done.31, bf16[256,768]{1,0:T(8,128)(2,1)} %get-tuple-element.155.g_own, ...), custom_call_target="tpu_custom_call" | custom-call | flops 70000001024 | bytes 1000000 | tf_op jit(solution)/shard_map/feed_weights/pallas_call | solution.py:845
  199.4 22.6 %attend_back.3 = (bf16[2,256,384]{2,1,0:T(8,128)(2,1)}, f32[4,256,384]{2,1,0:T(8,128)}, bf16[4,256,384]{2,1,0:T(8,128)(2,1)}) custom-call(s32[4]{0:T(128)} %pad_add_fusion.1.sc, s32[8,2]{1,0:T(8,128)} %copy.48.span, bf16[4,256,384]{2,1,0:T(8,128)(2,1)} %get-tuple-element.134.q, s32[8,1,256]{2,1,0:T(1,128)} %bitcast.69, ...), custom_call_target="tpu_custom_call" | custom-call | flops 219999993856 | bytes 1000000 | tf_op jit(solution)/shard_map/attend_back/pallas_call | solution.py:824
  228.1 5.8 %project_weights.1 = (f32[4,96,768]{2,1,0:T(8,128)}, bf16[4,96,768]{2,1,0:T(8,128)(2,1)}, f32[8,768]{1,0:T(8,128)}, bf16[4,256,768]{2,1,0:T(8,128)(2,1)}) custom-call(s32[4]{0:T(128)} %pad_add_fusion.1.sc, bf16[256,768]{1,0:T(8,128)(2,1)} %bitcast.85, bf16[256,768]{1,0:T(8,128)(2,1)} %copy-done.30, bf16[256,768]{1,0:T(8,128)(2,1)} %copy-done.29, ...), custom_call_target="tpu_custom_call" | custom-call | flops 60000002048 | bytes 1000000 | tf_op jit(solution)/shard_map/project_weights/pallas_call | solution.py:873
  234.0 3.4 spread_feed.1
  245.8 2.9 collective-permute-start.44
  248.8 4.2 %collective-permute-done.51 = bf16[200,768]{1,0:T(8,128)(2,1)S(1)} collective-permute-done((bf16[200,768]{1,0:T(8,128)(2,1)}, bf16[200,768]{1,0:T(8,128)(2,1)S(1)}, u32[]{:S(2)}, u32[]{:S(2)}) %collective-permute-start.51) | collective-permute-done | bytes 307232 | tf_op jit(solution)/shard_map/ppermute | solution.py:20
  253.0 4.2 %project_back.1 = (f32[256,768]{1,0:T(8,128)}, bf16[256,768]{1,0:T(8,128)(2,1)}, bf16[256,768]{1,0:T(8,128)(2,1)}, bf16[256,768]{1,0:T(8,128)(2,1)}) custom-call(s32[4]{0:T(128)} %pad_add_fusion.1.sc, bf16[4,256,768]{2,1,0:T(8,128)(2,1)} %get-tuple-element.194.both, bf16[768,768]{1,0:T(8,128)(2,1)} %get-tuple-element.195.w, ...), custom_call_target="tpu_custom_call" | custom-call | flops 40000000000 | bytes 1000000 | tf_op jit(solution)/shard_map/project_back/pallas_call | solution.py:890
  257.2 3.8 %collective-permute-done.52 = bf16[200,768]{1,0:T(8,128)(2,1)S(1)} collective-permute-done((bf16[200,768]{1,0:T(8,128)(2,1)}, bf16[200,768]{1,0:T(8,128)(2,1)S(1)}, u32[]{:S(2)}, u32[]{:S(2)}) %collective-permute-start.52) | collective-permute-done | bytes 307232 | tf_op jit(solution)/shard_map/ppermute | solution.py:20
  261.0 15.4 %collective-permute-done.53 = bf16[200,768]{1,0:T(8,128)(2,1)S(1)} collective-permute-done((bf16[200,768]{1,0:T(8,128)(2,1)}, bf16[200,768]{1,0:T(8,128)(2,1)S(1)}, u32[]{:S(2)}, u32[]{:S(2)}) %collective-permute-start.53) | collective-permute-done | bytes 307232 | tf_op jit(solution)/shard_map/ppermute | solution.py:20
  278.0 4.7 %collective-permute-done.46 = bf16[104,768]{1,0:T(8,128)(2,1)S(1)} collective-permute-done((bf16[104,768]{1,0:T(8,128)(2,1)}, bf16[104,768]{1,0:T(8,128)(2,1)S(1)}, u32[]{:S(2)}, u32[]{:S(2)}) %collective-permute-start.46) | collective-permute-done | bytes 159776 | tf_op jit(solution)/shard_map/ppermute | solution.py:20
  286.5 4.3 %collective-permute-done.49 = bf16[104,768]{1,0:T(8,128)(2,1)S(1)} collective-permute-done((bf16[104,768]{1,0:T(8,128)(2,1)S(1)}, bf16[104,768]{1,0:T(8,128)(2,1)S(1)}, u32[]{:S(2)}, u32[]{:S(2)}) %collective-permute-start.49) | collective-permute-done | bytes 159776 | tf_op jit(solution)/shard_map/ppermute | solution.py:20
  293.6 8.7 %collective-permute-done.48 = bf16[104,768]{1,0:T(8,128)(2,1)S(1)} collective-permute-done((bf16[104,768]{1,0:T(8,128)(2,1)S(1)}, bf16[104,768]{1,0:T(8,128)(2,1)S(1)}, u32[]{:S(2)}, u32[]{:S(2)}) %collective-permute-start.48) | collective-permute-done | bytes 159776 | tf_op jit(solution)/shard_map/ppermute | solution.py:20
  307.2 8.3 %collective-permute-done.55 = bf16[296,768]{1,0:T(8,128)(2,1)S(1)} collective-permute-done((bf16[296,768]{1,0:T(8,128)(2,1)S(1)}, bf16[296,768]{1,0:T(8,128)(2,1)S(1)}, u32[]{:S(2)}, u32[]{:S(2)}) %collective-permute-start.55) | collective-permute-done | bytes 454688 | tf_op jit(solution)/shard_map/ppermute | solution.py:20
  315.9 10.4 %collective-permute-done.56 = bf16[296,768]{1,0:T(8,128)(2,1)S(1)} collective-permute-done((bf16[296,768]{1,0:T(8,128)(2,1)S(1)}, bf16[296,768]{1,0:T(8,128)(2,1)S(1)}, u32[]{:S(2)}, u32[]{:S(2)}) %collective-permute-start.56) | collective-permute-done | bytes 454688 | tf_op jit(solution)/shard_map/ppermute | solution.py:20
  332.1 5.1 %finish_feed.1 = (f32[192,3072]{1,0:T(8,128)}, f32[768,768]{1,0:T(8,128)}, f32[1,768]{1,0:T(1,128)}, f32[192,768]{1,0:T(8,128)}) custom-call(s32[4]{0:T(128)} %pad_add_fusion.1.sc, bf16[4,296,768]{2,1,0:T(8,128)(2,1)} %copy-done, bf16[4,296,768]{2,1,0:T(8,128)(2,1)} %collective-permute-done.57.far), custom_call_target="tpu_custom_call" | custom-call | flops 49999998976 | bytes 1000000 | tf_op jit(solution)/shard_map/finish_feed/pallas_call | solution.py:914
  (214 shorter events, 100.7 us)
Async XLA Ops:
  6.5 20.9 %collective-permute-start.2 = (bf16[256,768]{1,0:T(8,128)(2,1)S(1)}, bf16[256,768]{1,0:T(8,128)(2,1)S(1)}, u32[]{:S(2)}, u32[]{:S(2)}) collective-permute-start(bf16[256,768]{1,0:T(8,128)(2,1)S(1)} %bitcast.86), channel_id=1, source_target_pairs={{0,24},{4,28},{8,16},{12,20},{16,8},{20,12},{24,0},{28,4},{1,25},{... | collective-permute-start | bytes 1179656 | tf_op jit(solution)/shard_map/ppermute | solution.py:20
  7.0 20.6 %collective-permute-start.1 = (bf16[256,768]{1,0:T(8,128)(2,1)S(1)}, bf16[256,768]{1,0:T(8,128)(2,1)S(1)}, u32[]{:S(2)}, u32[]{:S(2)}) collective-permute-start(bf16[256,768]{1,0:T(8,128)(2,1)S(1)} %bitcast.87), channel_id=1, source_target_pairs={{0,16},{4,20},{8,24},{12,28},{16,0},{20,4},{24,8},{28,12},{1,17},{... | collective-permute-start | bytes 1179656 | tf_op jit(solution)/shard_map/ppermute | solution.py:20
  8.5 22.9 %collective-permute-start = (bf16[256,768]{1,0:T(8,128)(2,1)S(1)}, bf16[256,768]{1,0:T(8,128)(2,1)S(1)}, u32[]{:S(2)}, u32[]{:S(2)}) collective-permute-start(bf16[256,768]{1,0:T(8,128)(2,1)S(1)} %bitcast.88), channel_id=1, source_target_pairs={{0,8},{4,12},{8,0},{12,4},{16,24},{20,28},{24,16},{28,20},{1,9},{5... | collective-permute-start | bytes 1179656 | tf_op jit(solution)/shard_map/ppermute | solution.py:20
  15.1 22.0 %collective-permute-start.9 = (bf16[192,384]{1,0:T(8,128)(2,1)}, bf16[192,384]{1,0:T(8,128)(2,1)S(1)}, u32[]{:S(2)}, u32[]{:S(2)}) collective-permute-start(bf16[192,384]{1,0:T(8,128)(2,1)} %get-tuple-element.129), channel_id=1, source_target_pairs={{0,3},{1,2},{2,1},{3,0},{4,7},{5,6},{6,5},{7,4},{8,11},{9,10},{10,... | collective-permute-start | bytes 442376 | tf_op jit(solution)/shard_map/ppermute | solution.py:20
  41.1 19.1 %collective-permute-start.17 = (bf16[4,192,384]{2,1,0:T(8,128)(2,1)S(1)}, bf16[4,192,384]{2,1,0:T(8,128)(2,1)S(1)}, u32[]{:S(2)}, u32[]{:S(2)}) collective-permute-start(bf16[4,192,384]{2,1,0:T(8,128)(2,1)S(1)} %pad_maximum_fusion.3.i0), channel_id=1, source_target_pairs={{0,8},{4,12},{8,0},{12,4},{16,24},{20,28},{24,16},{28,20},{1,9},{5... | collective-permute-start | bytes 1769480 | tf_op jit(solution)/shard_map/ppermute | solution.py:20
  41.7 34.2 %collective-permute-start.16 = (bf16[192,768]{1,0:T(8,128)(2,1)}, bf16[192,768]{1,0:T(8,128)(2,1)}, u32[]{:S(2)}, u32[]{:S(2)}) collective-permute-start(bf16[192,768]{1,0:T(8,128)(2,1)} %get-tuple-element.140.refs_0_), channel_id=1, source_target_pairs={{0,3},{1,2},{2,1},{3,0},{4,7},{5,6},{6,5},{7,4},{8,11},{9,10},{10,... | collective-permute-start | bytes 884744 | tf_op jit(solution)/shard_map/ppermute | solution.py:20
  41.7 34.2 %collective-permute-start.15 = (bf16[192,768]{1,0:T(8,128)(2,1)}, bf16[192,768]{1,0:T(8,128)(2,1)}, u32[]{:S(2)}, u32[]{:S(2)}) collective-permute-start(bf16[192,768]{1,0:T(8,128)(2,1)} %get-tuple-element.140.refs_0_), channel_id=1, source_target_pairs={{0,2},{1,3},{2,0},{3,1},{4,6},{5,7},{6,4},{7,5},{8,10},{9,11},{10,... | collective-permute-start | bytes 884744 | tf_op jit(solution)/shard_map/ppermute | solution.py:20
  45.4 30.5 %collective-permute-start.14 = (bf16[192,768]{1,0:T(8,128)(2,1)}, bf16[192,768]{1,0:T(8,128)(2,1)}, u32[]{:S(2)}, u32[]{:S(2)}) collective-permute-start(bf16[192,768]{1,0:T(8,128)(2,1)} %get-tuple-element.140.refs_0_), channel_id=1, source_target_pairs={{0,1},{1,0},{2,3},{3,2},{4,5},{5,4},{6,7},{7,6},{8,9},{9,8},{10,11... | collective-permute-start | bytes 884744 | tf_op jit(solution)/shard_map/ppermute | solution.py:20
  45.4 17.9 %collective-permute-start.18 = (bf16[4,192,384]{2,1,0:T(8,128)(2,1)S(1)}, bf16[4,192,384]{2,1,0:T(8,128)(2,1)S(1)}, u32[]{:S(2)}, u32[]{:S(2)}) collective-permute-start(bf16[4,192,384]{2,1,0:T(8,128)(2,1)S(1)} %pad_maximum_fusion.3.i0), channel_id=1, source_target_pairs={{0,16},{4,20},{8,24},{12,28},{16,0},{20,4},{24,8},{28,12},{1,17},{... | collective-permute-start | bytes 1769480 | tf_op jit(solution)/shard_map/ppermute | solution.py:20
  60.2 21.3 %collective-permute-start.13 = (bf16[256,192]{1,0:T(8,128)(2,1)S(1)}, bf16[256,192]{1,0:T(8,128)(2,1)S(1)}, u32[]{:S(2)}, u32[]{:S(2)}) collective-permute-start(bf16[256,192]{1,0:T(8,128)(2,1)S(1)} %get-tuple-element.235), channel_id=1, source_target_pairs={{0,24},{4,28},{8,16},{12,20},{16,8},{20,12},{24,0},{28,4},{1,25},{... | collective-permute-start | bytes 294920 | tf_op jit(solution)/shard_map/ppermute | solution.py:20
  81.5 17.0 %collective-permute-start.20 = (bf16[4,96,768]{2,1,0:T(8,128)(2,1)}, bf16[4,96,768]{2,1,0:T(8,128)(2,1)S(1)}, u32[]{:S(2)}, u32[]{:S(2)}) collective-permute-start(bf16[4,96,768]{2,1,0:T(8,128)(2,1)} %get-tuple-element.145.own), channel_id=1, source_target_pairs={{0,4},{4,0},{8,12},{12,8},{16,20},{20,16},{24,28},{28,24},{1,5},{5... | collective-permute-start | bytes 1769480 | tf_op jit(solution)/shard_map/ppermute | solution.py:20
  81.5 17.0 %collective-permute-start.12 = (bf16[256,192]{1,0:T(8,128)(2,1)S(1)}, bf16[256,192]{1,0:T(8,128)(2,1)S(1)}, u32[]{:S(2)}, u32[]{:S(2)}) collective-permute-start(bf16[256,192]{1,0:T(8,128)(2,1)S(1)} %get-tuple-element.236), channel_id=1, source_target_pairs={{0,16},{4,20},{8,24},{12,28},{16,0},{20,4},{24,8},{28,12},{1,17},{... | collective-permute-start | bytes 294920 | tf_op jit(solution)/shard_map/ppermute | solution.py:20
  84.6 18.6 %collective-permute-start.22 = (bf16[4,96,768]{2,1,0:T(8,128)(2,1)}, bf16[4,96,768]{2,1,0:T(8,128)(2,1)S(1)}, u32[]{:S(2)}, u32[]{:S(2)}) collective-permute-start(bf16[4,96,768]{2,1,0:T(8,128)(2,1)} %get-tuple-element.149.o0), channel_id=1, source_target_pairs={{0,8},{4,12},{8,0},{12,4},{16,24},{20,28},{24,16},{28,20},{1,9},{5... | collective-permute-start | bytes 1769480 | tf_op jit(solution)/shard_map/ppermute | solution.py:20
  97.1 17.6 %collective-permute-start.24 = (bf16[4,96,768]{2,1,0:T(8,128)(2,1)S(1)}, bf16[4,96,768]{2,1,0:T(8,128)(2,1)S(1)}, u32[]{:S(2)}, u32[]{:S(2)}) collective-permute-start(bf16[4,96,768]{2,1,0:T(8,128)(2,1)S(1)} %collective-permute-done.23.o2), channel_id=1, source_target_pairs={{0,8},{4,12},{8,0},{12,4},{16,24},{20,28},{24,16},{28,20},{1,9},{5... | collective-permute-start | bytes 1769480 | tf_op jit(solution)/shard_map/ppermute | solution.py:20
  160.0 28.3 %collective-permute-start.35 = (bf16[4,96,768]{2,1,0:T(8,128)(2,1)}, bf16[4,96,768]{2,1,0:T(8,128)(2,1)}, u32[]{:S(2)}, u32[]{:S(2)}) collective-permute-start(bf16[4,96,768]{2,1,0:T(8,128)(2,1)} %get-tuple-element.181), channel_id=1, source_target_pairs={{0,8},{4,12},{8,0},{12,4},{16,24},{20,28},{24,16},{28,20},{1,9},{5... | collective-permute-start | bytes 1769480 | tf_op jit(solution)/shard_map/ppermute | solution.py:20
  160.7 27.6 %collective-permute-start.36 = (bf16[4,104,768]{2,1,0:T(8,128)(2,1)}, bf16[4,104,768]{2,1,0:T(8,128)(2,1)}, u32[]{:S(2)}, u32[]{:S(2)}) collective-permute-start(bf16[4,104,768]{2,1,0:T(8,128)(2,1)} %get-tuple-element.182), channel_id=1, source_target_pairs={{0,16},{4,20},{8,24},{12,28},{16,0},{20,4},{24,8},{28,12},{1,17},{... | collective-permute-start | bytes 1916936 | tf_op jit(solution)/shard_map/ppermute | solution.py:20
  164.0 24.3 %collective-permute-start.32 = (bf16[96,768]{1,0:T(8,128)(2,1)}, bf16[96,768]{1,0:T(8,128)(2,1)}, u32[]{:S(2)}, u32[]{:S(2)}) collective-permute-start(bf16[96,768]{1,0:T(8,128)(2,1)} %get-tuple-element.176), channel_id=1, source_target_pairs={{0,1},{1,0},{2,3},{3,2},{4,5},{5,4},{6,7},{7,6},{8,9},{9,8},{10,11... | collective-permute-start | bytes 442376 | tf_op jit(solution)/shard_map/ppermute | solution.py:20
  165.7 22.6 %collective-permute-start.33 = (bf16[96,768]{1,0:T(8,128)(2,1)}, bf16[96,768]{1,0:T(8,128)(2,1)}, u32[]{:S(2)}, u32[]{:S(2)}) collective-permute-start(bf16[96,768]{1,0:T(8,128)(2,1)} %get-tuple-element.177), channel_id=1, source_target_pairs={{0,2},{1,3},{2,0},{3,1},{4,6},{5,7},{6,4},{7,5},{8,10},{9,11},{10,... | collective-permute-start | bytes 442376 | tf_op jit(solution)/shard_map/ppermute | solution.py:20
  166.0 22.3 %collective-permute-start.34 = (bf16[96,768]{1,0:T(8,128)(2,1)}, bf16[96,768]{1,0:T(8,128)(2,1)}, u32[]{:S(2)}, u32[]{:S(2)}) collective-permute-start(bf16[96,768]{1,0:T(8,128)(2,1)} %get-tuple-element.178), channel_id=1, source_target_pairs={{0,3},{1,2},{2,1},{3,0},{4,7},{5,6},{6,5},{7,4},{8,11},{9,10},{10,... | collective-permute-start | bytes 442376 | tf_op jit(solution)/shard_map/ppermute | solution.py:20
  195.2 28.4 %collective-permute-start.37 = (bf16[4,200,768]{2,1,0:T(8,128)(2,1)}, bf16[4,200,768]{2,1,0:T(8,128)(2,1)}, u32[]{:S(2)}, u32[]{:S(2)}) collective-permute-start(bf16[4,200,768]{2,1,0:T(8,128)(2,1)} %get-tuple-element.189), channel_id=1, source_target_pairs={{0,8},{4,12},{8,0},{12,4},{16,24},{20,28},{24,16},{28,20},{1,9},{5... | collective-permute-start | bytes 3686408 | tf_op jit(solution)/shard_map/ppermute | solution.py:20
  196.6 28.1 %collective-permute-start.38 = (bf16[4,200,768]{2,1,0:T(8,128)(2,1)}, bf16[4,200,768]{2,1,0:T(8,128)(2,1)}, u32[]{:S(2)}, u32[]{:S(2)}) collective-permute-start(bf16[4,200,768]{2,1,0:T(8,128)(2,1)} %get-tuple-element.190), channel_id=1, source_target_pairs={{0,16},{4,20},{8,24},{12,28},{16,0},{20,4},{24,8},{28,12},{1,17},{... | collective-permute-start | bytes 3686408 | tf_op jit(solution)/shard_map/ppermute | solution.py:20
  240.0 21.0 %collective-permute-start.52 = (bf16[200,768]{1,0:T(8,128)(2,1)}, bf16[200,768]{1,0:T(8,128)(2,1)S(1)}, u32[]{:S(2)}, u32[]{:S(2)}) collective-permute-start(bf16[200,768]{1,0:T(8,128)(2,1)} %get-tuple-element.218), channel_id=1, source_target_pairs={{0,2},{1,3},{2,0},{3,1},{4,6},{5,7},{6,4},{7,5},{8,10},{9,11},{10,... | collective-permute-start | bytes 921608 | tf_op jit(solution)/shard_map/ppermute | solution.py:20
  240.0 36.4 %collective-permute-start.53 = (bf16[200,768]{1,0:T(8,128)(2,1)}, bf16[200,768]{1,0:T(8,128)(2,1)S(1)}, u32[]{:S(2)}, u32[]{:S(2)}) collective-permute-start(bf16[200,768]{1,0:T(8,128)(2,1)} %get-tuple-element.219), channel_id=1, source_target_pairs={{0,3},{1,2},{2,1},{3,0},{4,7},{5,6},{6,5},{7,4},{8,11},{9,10},{10,... | collective-permute-start | bytes 921608 | tf_op jit(solution)/shard_map/ppermute | solution.py:20
  245.8 31.5 %collective-permute-start.44 = (bf16[104,768]{1,0:T(8,128)(2,1)}, bf16[104,768]{1,0:T(8,128)(2,1)S(1)}, u32[]{:S(2)}, u32[]{:S(2)}) collective-permute-start(bf16[104,768]{1,0:T(8,128)(2,1)} %get-tuple-element.206), channel_id=1, source_target_pairs={{0,1},{1,0},{2,3},{3,2},{4,5},{5,4},{6,7},{7,6},{8,9},{9,8},{10,11... | collective-permute-start | bytes 479240 | tf_op jit(solution)/shard_map/ppermute | solution.py:20
  248.8 29.3 %collective-permute-start.45 = (bf16[104,768]{1,0:T(8,128)(2,1)}, bf16[104,768]{1,0:T(8,128)(2,1)S(1)}, u32[]{:S(2)}, u32[]{:S(2)}) collective-permute-start(bf16[104,768]{1,0:T(8,128)(2,1)} %get-tuple-element.207), channel_id=1, source_target_pairs={{0,2},{1,3},{2,0},{3,1},{4,6},{5,7},{6,4},{7,5},{8,10},{9,11},{10,... | collective-permute-start | bytes 479240 | tf_op jit(solution)/shard_map/ppermute | solution.py:20
  253.0 29.8 %collective-permute-start.46 = (bf16[104,768]{1,0:T(8,128)(2,1)}, bf16[104,768]{1,0:T(8,128)(2,1)S(1)}, u32[]{:S(2)}, u32[]{:S(2)}) collective-permute-start(bf16[104,768]{1,0:T(8,128)(2,1)} %get-tuple-element.208), channel_id=1, source_target_pairs={{0,3},{1,2},{2,1},{3,0},{4,7},{5,6},{6,5},{7,4},{8,11},{9,10},{10,... | collective-permute-start | bytes 479240 | tf_op jit(solution)/shard_map/ppermute | solution.py:20
  276.4 26.2 %collective-permute-start.41 = (bf16[256,768]{1,0:T(8,128)(2,1)}, bf16[256,768]{1,0:T(8,128)(2,1)S(1)}, u32[]{:S(2)}, u32[]{:S(2)}) collective-permute-start(bf16[256,768]{1,0:T(8,128)(2,1)} %get-tuple-element.203), channel_id=1, source_target_pairs={{0,8},{4,12},{8,0},{12,4},{16,24},{20,28},{24,16},{28,20},{1,9},{5... | collective-permute-start | bytes 1179656 | tf_op jit(solution)/shard_map/ppermute | solution.py:20
  277.1 27.0 %collective-permute-start.42 = (bf16[256,768]{1,0:T(8,128)(2,1)}, bf16[256,768]{1,0:T(8,128)(2,1)S(1)}, u32[]{:S(2)}, u32[]{:S(2)}) collective-permute-start(bf16[256,768]{1,0:T(8,128)(2,1)} %get-tuple-element.204), channel_id=1, source_target_pairs={{0,16},{4,20},{8,24},{12,28},{16,0},{20,4},{24,8},{28,12},{1,17},{... | collective-permute-start | bytes 1179656 | tf_op jit(solution)/shard_map/ppermute | solution.py:20
  283.2 19.1 %collective-permute-start.48 = (bf16[104,768]{1,0:T(8,128)(2,1)S(1)}, bf16[104,768]{1,0:T(8,128)(2,1)S(1)}, u32[]{:S(2)}, u32[]{:S(2)}) collective-permute-start(bf16[104,768]{1,0:T(8,128)(2,1)S(1)} %add_convert_fusion.1), channel_id=1, source_target_pairs={{0,16},{4,20},{8,24},{12,28},{16,0},{20,4},{24,8},{28,12},{1,17},{... | collective-permute-start | bytes 479240 | tf_op jit(solution)/shard_map/ppermute | solution.py:20
  285.0 17.3 %collective-permute-start.47 = (bf16[104,768]{1,0:T(8,128)(2,1)S(1)}, bf16[104,768]{1,0:T(8,128)(2,1)S(1)}, u32[]{:S(2)}, u32[]{:S(2)}) collective-permute-start(bf16[104,768]{1,0:T(8,128)(2,1)S(1)} %add_convert_fusion.1), channel_id=1, source_target_pairs={{0,8},{4,12},{8,0},{12,4},{16,24},{20,28},{24,16},{28,20},{1,9},{5... | collective-permute-start | bytes 479240 | tf_op jit(solution)/shard_map/ppermute | solution.py:20
  302.4 24.3 %collective-permute-start.50 = (bf16[4,104,768]{2,1,0:T(8,128)(2,1)S(1)}, bf16[4,104,768]{2,1,0:T(8,128)(2,1)S(1)}, u32[]{:S(2)}, u32[]{:S(2)}) collective-permute-start(bf16[4,104,768]{2,1,0:T(8,128)(2,1)S(1)} %pad_maximum_fusion.2.near), channel_id=1, source_target_pairs={{0,4},{4,0},{8,12},{12,8},{16,20},{20,16},{24,28},{28,24},{1,5},{5... | collective-permute-start | bytes 1916936 | tf_op jit(solution)/shard_map/ppermute | solution.py:20
  304.1 22.3 %collective-permute-start.56 = (bf16[296,768]{1,0:T(8,128)(2,1)S(1)}, bf16[296,768]{1,0:T(8,128)(2,1)S(1)}, u32[]{:S(2)}, u32[]{:S(2)}) collective-permute-start(bf16[296,768]{1,0:T(8,128)(2,1)S(1)} %get-tuple-element.234), channel_id=1, source_target_pairs={{0,24},{4,28},{8,16},{12,20},{16,8},{20,12},{24,0},{28,4},{1,25},{... | collective-permute-start | bytes 1363976 | tf_op jit(solution)/shard_map/ppermute | solution.py:20
  (66 other events, 538.2 us)
